TPU v7x, 256 devices: a whole 4x4x8 slice. The times are simulated.
256 devices in a mesh: gx: 2 (over core), gy: 2 (over x_hi), gz: 64 (over z, y, x_lo).
Axes of the slice: x: 4 (x_hi: 2, x_lo: 2; x = x_hi * 2 + x_lo), y: 4, z: 8, core: 2. Of those that a mesh axis runs over, the one named last changes fastest.
Arguments:
- zvecs: bfloat16 [512, 3, 64, 4096], P(('gx', 'gy', 'gz')), may hold values from -0.0546875 to 0.0546875
- counts: int32 [512], P(('gx', 'gy', 'gz')), may hold values from 16 to 64
- adjacency: int32 [512, 6], P(('gx', 'gy', 'gz')), may hold values from -1 to 511, as said below
- mat_id: int32 [512], replicated, may hold values from 0 to 15
- shear: float32 [16], replicated, may hold values from 0.25 to 4
- ratio: float32 [16], replicated, may hold values from 0.5 to 2
- owner_map: int32 [4, 128], P(('gx', 'gy')), may hold values from 0 to 127, each once within a row
Outputs:
- agglom: float32 [4, 128, 7, 4096], P(('gx', 'gy'), 'gz')
Inputs may be any that keep to these rules, and one draw needn't show every extreme that they name: For each direction d, adjacency[i, 2 d + 1] = j names a subdomain of the next device along the d-th mesh axis (gx, gy, gz, device index (ix * 2 + iy) * 64 + iz holding subdomains index * 2 to index * 2 + 1) and then adjacency[j, 2 d] = i; -1 exactly where the device is the last (for 2 d + 1) or first (for 2 d) along that axis.
All inputs are finite; a program needn't handle non-finite values.
Results may differ from a plain program's by a relative error of at most 0.0003.
Values may be sent and summed in bfloat16 or wider, within the bound.
A program may use at most 192 MiB of HBM per device.

v0:
```python
import jax
import jax.numpy as jnp
from jax import lax
from jax.sharding import PartitionSpec as P

BX = 16
BY = 16
BZ = 16


def extended(shard, sides, width):
    for axis, dim in sides:
        peers, length = (lax.axis_size(axis), shard.shape[dim])
        up = [(i, (i + 1) % peers) for i in range(peers - 1)]
        down = [(j, i) for i, j in up]
        last = lax.slice_in_dim(shard, length - width, length, axis=dim)
        initial = lax.slice_in_dim(shard, 0, width, axis=dim)
        before = lax.ppermute(last, axis, up)
        after = lax.ppermute(initial, axis, down)
        shard = jnp.concatenate([before, shard, after], axis=dim)
    return shard


def stencil(u, coef):
    cell = lax.iota(jnp.int32, BX * BY * BZ)
    zpos = cell % BZ
    ypos = cell // BZ % BY
    xpos = cell // (BY * BZ)
    plain = u.astype(jnp.float32)
    total = jnp.zeros(plain.shape, jnp.float32)
    lead = [(0, 0)] * (u.ndim - 1)
    for direction, stride, where_at, extent in (
        (0, BY * BZ, xpos, BX),
        (1, BZ, ypos, BY),
        (2, 1, zpos, BZ),
    ):
        upper = jnp.pad(plain[..., stride:], lead + [(0, stride)])
        upper = jnp.where(where_at < extent - 1, upper, jnp.zeros((), jnp.float32))
        lower = jnp.pad(plain[..., :-stride], lead + [(stride, 0)])
        lower = jnp.where(where_at > 0, lower, jnp.zeros((), jnp.float32))
        total = total + coef[..., direction][..., None, None] * (2.0 * plain - upper - lower)
    return total


def face(u, direction, high):
    lead = u.shape[:-1]
    block = u.reshape(lead + (BX, BY, BZ))
    if direction == 0:
        return block[..., high * (BX - 1), :, :].reshape(lead + (BY * BZ,))
    if direction == 1:
        return block[..., :, high * (BY - 1), :].reshape(lead + (BX * BZ,))
    return block[..., :, :, high * (BZ - 1)].reshape(lead + (BX * BY,))


def coefficients(ids, shear, ratio):
    onehot = (ids[..., None] == lax.iota(jnp.int32, shear.shape[0])).astype(jnp.float32)
    modulus = jnp.sum(onehot * shear, -1)
    excess = jnp.sum(onehot * ratio, -1)
    unit = (lax.iota(jnp.int32, 3)[:, None] == lax.iota(jnp.int32, 3)[None, :]).astype(jnp.float32)
    return modulus[..., None, None] * (1.0 + excess[..., None, None] * unit)


def neighbour_layers(both, direction):
    if direction == 0:
        return extended(both, (("gx", 0),), 1)
    if direction == 1:
        return extended(both, (("gy", 0),), 1)
    return extended(both, (("gz", 0),), 1)


def per_device(zvecs, counts, adjacency, mat_id, shear, ratio, owner_map):
    subs = zvecs.shape[0]
    nvec = zvecs.shape[2]
    keep = lax.iota(jnp.int32, nvec)[None, :] < counts[:, None]
    masked = jnp.where(keep[:, None, :, None], zvecs, jnp.zeros((), zvecs.dtype))
    device = lax.axis_index(("gx", "gy", "gz"))
    own_ids = lax.dynamic_slice_in_dim(mat_id, device * subs, subs)
    coef = coefficients(own_ids, shear, ratio)
    applied = stencil(masked, coef).astype(jnp.bfloat16)
    blocks = [jnp.einsum("scvx,scwx->svw", masked, applied, preferred_element_type=jnp.float32)]
    valid = (adjacency >= 0).astype(jnp.float32)
    local = jnp.where(adjacency >= 0, adjacency % subs, 0)
    far_coef = coefficients(jnp.take(mat_id, jnp.maximum(adjacency, 0)), shear, ratio)

    def couple(near_face, far_face, slot):
        direction = slot // 2
        weight = (
            -jnp.sqrt(coef[:, :, direction] * far_coef[:, slot, :, direction])
            * valid[:, slot : slot + 1]
        )
        inner = jnp.einsum(
            "scvx,scwx->scvw", near_face, far_face, preferred_element_type=jnp.float32
        )
        return jnp.sum(weight[:, :, None, None] * inner, 1)

    for direction in range(3):
        both = jnp.stack([face(masked, direction, 0), face(masked, direction, 1)], 0)
        padded = neighbour_layers(both, direction)
        below = jnp.take(padded[0], local[:, 2 * direction], axis=0)
        above = jnp.take(padded[3], local[:, 2 * direction + 1], axis=0)
        blocks.append(couple(both[0], below, 2 * direction))
        blocks.append(couple(both[1], above, 2 * direction + 1))
    rows = jnp.stack(blocks, 1).reshape(subs, 7, nvec * nvec)
    column = owner_map[0]
    position = lax.axis_index("gz")
    places = jnp.take(column, position * subs + lax.iota(jnp.int32, subs))
    peers = lax.axis_size("gz")
    send = jnp.zeros((peers, subs) + rows.shape[1:], jnp.float32)
    send = send.at[places // subs, places % subs].set(rows)
    arrived = lax.all_to_all(send, "gz", split_axis=0, concat_axis=0, tiled=True)
    agglom = jnp.sum(arrived, 0)[None]
    return agglom


def solution(mesh):
    placed = (
        P(("gx", "gy", "gz"), None, None, None),
        P(("gx", "gy", "gz")),
        P(("gx", "gy", "gz"), None),
        P(),
        P(),
        P(),
        P(("gx", "gy"), None),
    )
    return jax.shard_map(
        per_device,
        mesh=mesh,
        in_specs=placed,
        out_specs=P(("gx", "gy"), "gz", None, None),
        check_vma=False,
    )
```

profile of v0, /device:TPU:4, one launch (start us, length us, event | category | flops | bytes accessed | tf_op | source)
XLA Modules:
  0.0 474.4 jit_solution(2204951519305328256)
XLA Ops:
  0.0 6.6 %copy.49 = bf16[2,3,64,4096]{2,3,1,0:T(8,128)(2,1)} copy(bf16[2,3,64,4096]{3,2,1,0:T(8,128)(2,1)} %param.9) | data formatting | bytes 6291456 | tf_op args[0]
  7.4 3.2 broadcast_select_fusion
  10.6 1.5 fusion.78
  12.1 3.9 collective-permute-start.4
  16.0 1.3 collective-permute-start.5
  17.5 2.3 collective-permute-start
  19.8 1.3 collective-permute-start.1
  21.2 1.3 collective-permute-start.2
  22.5 8.9 %fusion.83 = (f32[2,3,64,4095]{2,3,1,0:T(8,128)}, f32[2,3,64,4095]{2,3,1,0:T(8,128)}) fusion(bf16[2,3,64,4096]{2,3,1,0:T(8,128)(2,1)S(1)} %broadcast_select_fusion), kind=kLoop, calls=%fused_computation.183 | loop fusion | bytes 25159680 | tf_op jit(solution)/shard_map/slice | solution.py:37
  31.5 8.9 %fusion.82 = (f32[2,3,64,4080]{2,3,1,0:T(8,128)}, f32[2,3,64,4080]{2,3,1,0:T(8,128)}) fusion(bf16[2,3,64,4096]{2,3,1,0:T(8,128)(2,1)S(1)} %broadcast_select_fusion), kind=kLoop, calls=%fused_computation.182 | loop fusion | bytes 25067520 | tf_op jit(solution)/shard_map/slice | solution.py:37
  40.4 8.5 %fusion.81 = (f32[2,3,64,3840]{2,3,1,0:T(8,128)}, f32[2,3,64,3840]{2,3,1,0:T(8,128)}) fusion(bf16[2,3,64,4096]{2,3,1,0:T(8,128)(2,1)S(1)} %broadcast_select_fusion), kind=kLoop, calls=%fused_computation.181 | loop fusion | bytes 23592960 | tf_op jit(solution)/shard_map/slice | solution.py:37
  52.0 29.3 %fusion.8 = f32[2,64,64]{2,1,0:T(8,128)S(1)} fusion(bf16[2,3,64,4096]{2,3,1,0:T(8,128)(2,1)} %copy-done.2, f32[2,3,64,4095]{2,3,1,0:T(8,128)} %get-tuple-element.33, f32[2,3,64,4095]{2,3,1,0:T(8,128)} %get-tuple-element.32, f32[2,3,64,4080]{2,3,1,0:T(8,128)} %get-tuple-element.31, f32[2,3,64,4080]{2,3,1,0:T(8,128)} %get-tuple-element.30, ...), kind=kOutput, calls=%fused_computation.25 | convolution fusion | flops 232783872 | bytes 40113224 | tf_op jit(solution)/shard_map/scvx,scwx->svw/dot_general | solution.py:80
  81.4 6.8 %collective-permute-start.3 = (bf16[1,2,3,64,256]{3,4,2,1,0:T(8,128)(2,1)S(1)}, bf16[1,2,3,64,256]{3,4,2,1,0:T(8,128)(2,1)}, u32[]{:S(2)}, u32[]{:S(2)}) collective-permute-start(bf16[1,2,3,64,256]{3,4,2,1,0:T(8,128)(2,1)S(1)} %bitcast.128), channel_id=1, source_target_pairs={{64,0},{65,1},{66,2},{67,3},{68,4},{69,5},{70,6},{71,7},{72,8},{73... | collective-permute-start | bytes 589832 | tf_op jit(solution)/shard_map/ppermute | solution.py:19
  88.3 2.3 gather_fusion.6
  90.6 1.3 fusion.6
  91.9 1.6 gather_fusion.7
  93.8 1.6 gather_fusion.2
  98.2 1.6 gather_fusion.5
  100.6 7.8 %broadcast_in_dim.92 = f32[64,2,7,4096]{3,2,1,0:T(8,128)} broadcast(f32[]{:T(128)} %constant.137.clone.1), dimensions={} | broadcast | bytes 14680068 | tf_op jit(solution)/shard_map/broadcast_in_dim | solution.py:108
  108.4 2.2 scatter_fusion
  110.6 21.6 %copy.66 = f32[64,2,7,4096]{3,1,2,0:T(2,128)S(1)} copy(f32[64,2,7,4096]{3,2,1,0:T(8,128)} %scatter_fusion) | data formatting | bytes 29360128 | tf_op jit(solution)/shard_map/scatter | solution.py:109
  132.3 335.0 %all_to_all.5 = f32[64,2,7,4096]{3,1,2,0:T(2,128)} all-to-all(f32[64,2,7,4096]{3,1,2,0:T(2,128)S(1)} %copy.66), channel_id=1, replica_groups=mesh['gx'=2,'gy'=2,'gz'=64] {'gz'}, dimensions={0} | all-to-all | bytes 29360128 | tf_op jit(solution)/shard_map/all_to_all | solution.py:110
  467.3 6.1 %reduce_sum.109 = f32[2,7,4096]{2,0,1:T(2,128)S(1)} reduce(f32[64,2,7,4096]{3,1,2,0:T(2,128)} %all_to_all.5, f32[]{:T(128)} %constant.137.clone.1), dimensions={0}, to_apply=%region_11.13 | reduce | flops 3612672 | bytes 14909444 | tf_op jit(solution)/shard_map/reduce_sum | solution.py:111
  473.5 0.9 copy.68
  (84 shorter events, 8.0 us)
Async XLA Ops:
  0.0 51.2 %copy-start = (s32[1,128]{1,0:T(1,128)S(1)}, s32[1,128]{1,0:T(1,128)}, u32[]{:S(2)}) copy-start(s32[1,128]{1,0:T(1,128)} %param.15) | copy-start | bytes 1540
  10.6 29.8 %copy-start.2 = (bf16[2,3,64,4096]{2,3,1,0:T(8,128)(2,1)}, bf16[2,3,64,4096]{2,3,1,0:T(8,128)(2,1)S(1)}, u32[]{:S(2)}) copy-start(bf16[2,3,64,4096]{2,3,1,0:T(8,128)(2,1)S(1)} %broadcast_select_fusion) | copy-start | bytes 9437188
  12.1 69.3 %collective-permute-start.4 = (bf16[1,2,3,64,256]{3,4,2,1,0:T(8,128)(2,1)S(1)}, bf16[1,2,3,64,256]{3,4,2,1,0:T(8,128)(2,1)}, u32[]{:S(2)}, u32[]{:S(2)}) collective-permute-start(bf16[1,2,3,64,256]{3,4,2,1,0:T(8,128)(2,1)S(1)} %bitcast.132), channel_id=1, source_target_pairs={{0,1},{1,2},{2,3},{3,4},{4,5},{5,6},{6,7},{7,8},{8,9},{9,10},{10,1... | collective-permute-start | bytes 589832 | tf_op jit(solution)/shard_map/ppermute | solution.py:18
  16.0 75.8 %collective-permute-start.5 = (bf16[1,2,3,64,256]{3,4,2,1,0:T(8,128)(2,1)S(1)}, bf16[1,2,3,64,256]{3,4,2,1,0:T(8,128)(2,1)}, u32[]{:S(2)}, u32[]{:S(2)}) collective-permute-start(bf16[1,2,3,64,256]{3,4,2,1,0:T(8,128)(2,1)S(1)} %bitcast.136), channel_id=1, source_target_pairs={{1,0},{2,1},{3,2},{4,3},{5,4},{6,5},{7,6},{8,7},{9,8},{10,9},{11,1... | collective-permute-start | bytes 589832 | tf_op jit(solution)/shard_map/ppermute | solution.py:19
  17.5 76.3 %collective-permute-start = (bf16[1,2,3,64,256]{3,4,2,1,0:T(8,128)(2,1)S(1)}, bf16[1,2,3,64,256]{3,4,2,1,0:T(8,128)(2,1)}, u32[]{:S(2)}, u32[]{:S(2)}) collective-permute-start(bf16[1,2,3,64,256]{3,4,2,1,0:T(8,128)(2,1)S(1)} %bitcast.130), channel_id=1, source_target_pairs={{0,128},{1,129},{2,130},{3,131},{4,132},{5,133},{6,134},{7,135},{8... | collective-permute-start | bytes 589832 | tf_op jit(solution)/shard_map/ppermute | solution.py:18
  19.8 76.0 %collective-permute-start.1 = (bf16[1,2,3,64,256]{3,4,2,1,0:T(8,128)(2,1)S(1)}, bf16[1,2,3,64,256]{3,4,2,1,0:T(8,128)(2,1)S(1)}, u32[]{:S(2)}, u32[]{:S(2)}) collective-permute-start(bf16[1,2,3,64,256]{3,4,2,1,0:T(8,128)(2,1)S(1)} %bitcast.134), channel_id=1, source_target_pairs={{128,0},{129,1},{130,2},{131,3},{132,4},{133,5},{134,6},{135,7},{1... | collective-permute-start | bytes 589832 | tf_op jit(solution)/shard_map/ppermute | solution.py:19
  21.2 75.9 %collective-permute-start.2 = (bf16[1,2,3,64,256]{3,4,2,1,0:T(8,128)(2,1)S(1)}, bf16[1,2,3,64,256]{3,4,2,1,0:T(8,128)(2,1)S(1)}, u32[]{:S(2)}, u32[]{:S(2)}) collective-permute-start(bf16[1,2,3,64,256]{3,4,2,1,0:T(8,128)(2,1)S(1)} %bitcast.126), channel_id=1, source_target_pairs={{0,64},{1,65},{2,66},{3,67},{4,68},{5,69},{6,70},{7,71},{8,72},{9,... | collective-permute-start | bytes 589832 | tf_op jit(solution)/shard_map/ppermute | solution.py:18
  40.3 8.6 %copy-start.4 = (s32[2,6]{1,0:T(2,128)S(1)}, s32[2,6]{1,0:T(2,128)}, u32[]{:S(2)}) copy-start(s32[2,6]{1,0:T(2,128)} %param.11) | copy-start | bytes 148
  40.3 8.7 %copy-start.3 = (s32[512]{0:T(512)S(1)}, s32[512]{0:T(512)}, u32[]{:S(2)}) copy-start(s32[512]{0:T(512)} %param.12) | copy-start | bytes 6148
  40.3 10.0 %copy-start.5 = (f32[16]{0:T(128)S(1)}, f32[16]{0:T(128)}, u32[]{:S(2)}) copy-start(f32[16]{0:T(128)} %param.14) | copy-start | bytes 196
  40.4 10.0 %copy-start.6 = (f32[16]{0:T(128)S(1)}, f32[16]{0:T(128)}, u32[]{:S(2)}) copy-start(f32[16]{0:T(128)} %param.13) | copy-start | bytes 196
  81.4 16.7 %collective-permute-start.3 = (bf16[1,2,3,64,256]{3,4,2,1,0:T(8,128)(2,1)S(1)}, bf16[1,2,3,64,256]{3,4,2,1,0:T(8,128)(2,1)}, u32[]{:S(2)}, u32[]{:S(2)}) collective-permute-start(bf16[1,2,3,64,256]{3,4,2,1,0:T(8,128)(2,1)S(1)} %bitcast.128), channel_id=1, source_target_pairs={{64,0},{65,1},{66,2},{67,3},{68,4},{69,5},{70,6},{71,7},{72,8},{73... | collective-permute-start | bytes 589832 | tf_op jit(solution)/shard_map/ppermute | solution.py:19
  132.3 342.1 %copy-start.1 = (s32[1,128]{1,0:T(1,128)S(1)}, s32[1,128]{1,0:T(1,128)}, u32[]{:S(2)}) copy-start(s32[1,128]{1,0:T(1,128)} %param.15) | copy-start | bytes 1540
where the time goes:
time: 477 us; the launch traced here: 474 us
  blocking collectives  335 us (70%)
  local copies, waits for them, and re-layouts  79.2 us (17%)
  matrix products  32 us (7%)
  starting transfers between devices  16.8 us (4%)
  other arithmetic  10.8 us (2%)
    all_to_all x1, blocking collectives, per_device(): lax.all_to_all(send, 'gz', split_axis=0, concat_axis=0, tiled=True)  335 us
    dot_general x1, matrix products, per_device(): jnp.einsum('scvx,scwx->svw', masked, applied, preferred_element_type=jnp....  29.3 us
    slice x3, local copies, waits for them, and re-layouts, stencil(): upper = jnp.pad(plain[..., stride:], lead + [(0, stride)])  26.3 us
    scatter x2, local copies, waits for them, and re-layouts, per_device(): send = send.at[places // subs, places % subs].set(rows)  23.9 us
  transfers between devices with their start and end apart: 6, of which 0 were waited for; matrix products, arithmetic and copies ran while one was open for 14% of the time, Pallas kernels for 0%

commit v1 on v0

--- a/solution.py
+++ b/solution.py
@@ -100,15 +100,19 @@
         above = jnp.take(padded[3], local[:, 2 * direction + 1], axis=0)
         blocks.append(couple(both[0], below, 2 * direction))
         blocks.append(couple(both[1], above, 2 * direction + 1))
-    rows = jnp.stack(blocks, 1).reshape(subs, 7, nvec * nvec)
+    rows = jnp.stack(blocks, 1)
+    peers = lax.axis_size("gz")
+    lines = nvec // peers
+    cut = rows.reshape(subs, 7, peers, lines * nvec).transpose(2, 1, 0, 3).reshape(peers, 7, subs * lines * nvec)
+    spread = lax.all_to_all(cut, "gz", split_axis=0, concat_axis=0, tiled=True)
+    spread = spread.reshape(peers, 7, subs, lines * nvec).transpose(0, 2, 1, 3).reshape(peers * subs, 7, lines * nvec)
     column = owner_map[0]
-    position = lax.axis_index("gz")
-    places = jnp.take(column, position * subs + lax.iota(jnp.int32, subs))
-    peers = lax.axis_size("gz")
-    send = jnp.zeros((peers, subs) + rows.shape[1:], jnp.float32)
-    send = send.at[places // subs, places % subs].set(rows)
-    arrived = lax.all_to_all(send, "gz", split_axis=0, concat_axis=0, tiled=True)
-    agglom = jnp.sum(arrived, 0)[None]
+    places = lax.iota(jnp.int32, column.shape[0])
+    inverse = jnp.sum(jnp.where(column[None, :] == places[:, None], places[None, :], 0), 1)
+    owned = jnp.take(spread, inverse, axis=0, mode="clip")
+    owned = owned.reshape(peers, subs, 7, lines * nvec).transpose(0, 2, 1, 3).reshape(peers, 7, subs * lines * nvec)
+    arrived = lax.all_to_all(owned, "gz", split_axis=0, concat_axis=0, tiled=True)
+    agglom = arrived.reshape(peers, 7, subs, lines * nvec).transpose(2, 1, 0, 3).reshape(1, subs, 7, nvec * nvec)
     return agglom
 
 

time: 477 us -> 151 us (0.32)
  blocking collectives: 335 us -> 45.7 us
  local copies, waits for them, and re-layouts: 79.2 us -> 49.1 us
  other arithmetic: 10.8 us -> 4.85 us
    all_to_all x1 -> x2, blocking collectives: 335 us -> 45.7 us  [the longest x1 28.4 us: per_device(): spread = lax.all_to_all(cut, 'gz', split_axis=0, concat_axis=0, tiled=True)]
    scatter x2 -> x0, local copies, waits for them, and re-layouts: 23.9 us -> none  [per_device(): send = send.at[places // subs, places % subs].set(rows)]
    broadcast_in_dim x2 -> x0, local copies, waits for them, and re-layouts: 8.69 us -> none  [the longest x1 7.82 us: per_device(): send = jnp.zeros((peers, subs) + rows.shape[1:], jnp.float32)]
    reduce_sum x1, other arithmetic: 6.06 us -> 0.1 us  [per_device(): jnp.sum(jnp.where(column[None, :] == places[:, None], places[None, :], 0)...]
  transfers between devices with their start and end apart: 6 -> 6, of which waited for: 0 -> 1; matrix products, arithmetic and copies ran while one was open for 14% -> 47% of each run, Pallas kernels for 0% -> 0%
where the time goes in v1:
time: 151 us
  local copies, waits for them, and re-layouts  49.1 us (33%)
  blocking collectives  45.7 us (30%)
  matrix products  31.6 us (21%)
  starting transfers between devices  17.9 us (12%)
  other arithmetic  4.85 us (3%)
    dot_general x1, matrix products, per_device(): jnp.einsum('scvx,scwx->svw', masked, applied, preferred_element_type=jnp....  28.9 us
    all_to_all x1, blocking collectives, per_device(): spread = lax.all_to_all(cut, 'gz', split_axis=0, concat_axis=0, tiled=True)  28.4 us
    slice x3, local copies, waits for them, and re-layouts, stencil(): upper = jnp.pad(plain[..., stride:], lead + [(0, stride)])  26.3 us
    all_to_all x1, blocking collectives, per_device(): lax.all_to_all(owned, 'gz', split_axis=0, concat_axis=0, tiled=True)  17.3 us
    ppermute x3, starting transfers between devices, extended(): after = lax.ppermute(initial, axis, down)  10.1 us
    ppermute x3, starting transfers between devices, extended(): before = lax.ppermute(last, axis, up)  7.76 us
    unnamed x20, local copies, waits for them, and re-layouts  6.79 us
    gather x3, local copies, waits for them, and re-layouts, per_device(): below = jnp.take(padded[0], local[:, 2 * direction], axis=0)  5.57 us
  transfers between devices with their start and end apart: 6, of which 1 were waited for; matrix products, arithmetic and copies ran while one was open for 47% of the time, Pallas kernels for 0%

profile of v1, /device:TPU:4, one launch (start us, length us, event | category | flops | bytes accessed | tf_op | source)
XLA Modules:
  0.0 150.8 jit_solution(9551873859310837414)
XLA Ops:
  0.0 6.6 %copy.72 = bf16[2,3,64,4096]{2,3,1,0:T(8,128)(2,1)} copy(bf16[2,3,64,4096]{3,2,1,0:T(8,128)(2,1)} %param.9) | data formatting | bytes 6291456 | tf_op args[0]
  7.3 3.2 %broadcast_select_fusion = bf16[2,3,64,4096]{2,3,1,0:T(8,128)(2,1)S(1)} fusion(bf16[2,3,64,4096]{2,3,1,0:T(8,128)(2,1)} %copy.72, pred[2,64]{1,0:T(4,128)(4,1)S(1)} %iota_compare_fusion.4), kind=kLoop, calls=%fused_computation.9 | loop fusion | flops 1572864 | bytes 6291584 | tf_op jit(solution)/shard_map/jit(_where)/select_n | solution.py:75
  10.7 2.6 %collective-permute-start = (bf16[1,2,3,64,256]{3,4,2,1,0:T(8,128)(2,1)S(1)}, bf16[1,2,3,64,256]{3,4,2,1,0:T(8,128)(2,1)}, u32[]{:S(2)}, u32[]{:S(2)}) collective-permute-start(bf16[1,2,3,64,256]{3,4,2,1,0:T(8,128)(2,1)S(1)} %bitcast.152), channel_id=1, source_target_pairs={{0,128},{1,129},{2,130},{3,131},{4,132},{5,133},{6,134},{7,135},{8... | collective-permute-start | bytes 589832 | tf_op jit(solution)/shard_map/ppermute | solution.py:18
  13.3 1.3 collective-permute-start.1
  14.8 1.3 collective-permute-start.2
  16.1 7.6 %collective-permute-start.3 = (bf16[1,2,3,64,256]{3,4,2,1,0:T(8,128)(2,1)S(1)}, bf16[1,2,3,64,256]{3,4,2,1,0:T(8,128)(2,1)}, u32[]{:S(2)}, u32[]{:S(2)}) collective-permute-start(bf16[1,2,3,64,256]{3,4,2,1,0:T(8,128)(2,1)S(1)} %bitcast.150), channel_id=1, source_target_pairs={{64,0},{65,1},{66,2},{67,3},{68,4},{69,5},{70,6},{71,7},{72,8},{73... | collective-permute-start | bytes 589832 | tf_op jit(solution)/shard_map/ppermute | solution.py:19
  23.6 1.2 fusion.76
  24.9 3.9 %collective-permute-start.4 = (bf16[1,2,3,64,256]{3,4,2,1,0:T(8,128)(2,1)S(1)}, bf16[1,2,3,64,256]{3,4,2,1,0:T(8,128)(2,1)}, u32[]{:S(2)}, u32[]{:S(2)}) collective-permute-start(bf16[1,2,3,64,256]{3,4,2,1,0:T(8,128)(2,1)S(1)} %bitcast.146), channel_id=1, source_target_pairs={{0,1},{1,2},{2,3},{3,4},{4,5},{5,6},{6,7},{7,8},{8,9},{9,10},{10,1... | collective-permute-start | bytes 589832 | tf_op jit(solution)/shard_map/ppermute | solution.py:18
  28.8 8.9 %fusion.81 = (f32[2,3,64,4095]{2,3,1,0:T(8,128)}, f32[2,3,64,4095]{2,3,1,0:T(8,128)}) fusion(bf16[2,3,64,4096]{2,3,1,0:T(8,128)(2,1)S(1)} %broadcast_select_fusion), kind=kLoop, calls=%fused_computation.177 | loop fusion | bytes 25159680 | tf_op jit(solution)/shard_map/slice | solution.py:37
  37.7 8.9 %fusion.80 = (f32[2,3,64,4080]{2,3,1,0:T(8,128)}, f32[2,3,64,4080]{2,3,1,0:T(8,128)}) fusion(bf16[2,3,64,4096]{2,3,1,0:T(8,128)(2,1)S(1)} %broadcast_select_fusion), kind=kLoop, calls=%fused_computation.176 | loop fusion | bytes 25067520 | tf_op jit(solution)/shard_map/slice | solution.py:37
  46.6 8.5 %fusion.79 = (f32[2,3,64,3840]{2,3,1,0:T(8,128)}, f32[2,3,64,3840]{2,3,1,0:T(8,128)}) fusion(bf16[2,3,64,4096]{2,3,1,0:T(8,128)(2,1)S(1)} %broadcast_select_fusion), kind=kLoop, calls=%fused_computation.175 | loop fusion | bytes 23592960 | tf_op jit(solution)/shard_map/slice | solution.py:37
  57.7 28.9 %fusion.9 = f32[2,7,64,64]{3,2,0,1:T(8,128)S(1)} fusion(bf16[2,3,64,4096]{2,3,1,0:T(8,128)(2,1)} %copy-done, f32[2,3,64,4095]{2,3,1,0:T(8,128)} %get-tuple-element.33, f32[2,3,64,4095]{2,3,1,0:T(8,128)} %get-tuple-element.32, f32[2,3,64,4080]{2,3,1,0:T(8,128)} %get-tuple-element.31, f32[2,3,64,4080]{2,3,1,0:T(8,128)} %get-tuple-element.30, ...), kind=kOutput, calls=%fused_computation.25 | convolution fusion | flops 232783872 | bytes 86499400 | tf_op jit(solution)/shard_map/scvx,scwx->svw/dot_general | solution.py:80
  86.6 1.3 collective-permute-start.5
  87.9 2.3 %gather_fusion.2 = bf16[2,3,64,256]{2,3,1,0:T(8,128)(2,1)} fusion(bf16[2,3,64,256]{2,3,1,0:T(8,128)(2,1)} %bitcast.10, s32[1024]{0:T(1024)S(1)} %pad_clamp_fusion.6), kind=kCustom, calls=%fused_computation.clone | custom fusion | bytes 393224 | tf_op jit(solution)/shard_map/jit(_take)/gather | solution.py:99
  90.3 1.3 fusion.2
  91.6 1.6 %gather_fusion.3 = bf16[2,3,64,256]{2,3,1,0:T(8,128)(2,1)S(1)} fusion(bf16[2,3,64,256]{2,3,1,0:T(8,128)(2,1)} %bitcast.15, s32[1024]{0:T(1024)S(1)} %pad_clamp_fusion.5), kind=kCustom, calls=%fused_computation.1.clone | custom fusion | bytes 393224 | tf_op jit(solution)/shard_map/jit(_take)/gather | solution.py:100
  93.5 1.6 %gather_fusion.4 = bf16[2,3,64,256]{2,3,1,0:T(8,128)(2,1)S(1)} fusion(bf16[2,3,64,256]{2,3,1,0:T(8,128)(2,1)} %bitcast.20, s32[1024]{0:T(1024)S(1)} %pad_clamp_fusion.4), kind=kCustom, calls=%fused_computation.2.clone | custom fusion | bytes 393224 | tf_op jit(solution)/shard_map/jit(_take)/gather | solution.py:99
  95.5 1.6 %gather_fusion.5 = bf16[2,3,64,256]{2,3,1,0:T(8,128)(2,1)S(1)} fusion(bf16[2,3,64,256]{2,3,1,0:T(8,128)(2,1)} %bitcast.25, s32[1024]{0:T(1024)S(1)} %pad_clamp_fusion.3), kind=kCustom, calls=%fused_computation.3.clone | custom fusion | bytes 393224 | tf_op jit(solution)/shard_map/jit(_take)/gather | solution.py:100
  97.5 1.6 %gather_fusion.6 = bf16[2,3,64,256]{2,3,1,0:T(8,128)(2,1)S(1)} fusion(bf16[2,3,64,256]{2,3,1,0:T(8,128)(2,1)} %bitcast.28, s32[1024]{0:T(1024)S(1)} %pad_clamp_fusion.2), kind=kCustom, calls=%fused_computation.4.clone | custom fusion | bytes 393224 | tf_op jit(solution)/shard_map/jit(_take)/gather | solution.py:99
  99.4 1.0 collective-permute-done.5
  102.0 28.4 %all_to_all.10 = f32[64,7,128]{2,1,0:T(8,128)S(1)} all-to-all(f32[64,7,128]{2,1,0:T(8,128)S(1)} %reshape.358), channel_id=1, replica_groups=mesh['gx'=2,'gy'=2,'gz'=64] {'gz'}, dimensions={0} | all-to-all | bytes 458752 | tf_op jit(solution)/shard_map/all_to_all | solution.py:107
  130.7 0.8 gather_fusion.1
  132.1 17.3 %all_to_all.11 = f32[64,7,128]{2,1,0:T(8,128)S(1)} all-to-all(f32[64,7,128]{2,1,0:T(8,128)S(1)} %copy.91), channel_id=1, replica_groups=mesh['gx'=2,'gy'=2,'gz'=64] {'gz'}, dimensions={0} | all-to-all | bytes 458752 | tf_op jit(solution)/shard_map/all_to_all | solution.py:114
  149.8 0.9 reshape.271
  (85 shorter events, 7.6 us)
Async XLA Ops:
  10.5 36.0 %copy-start = (bf16[2,3,64,4096]{2,3,1,0:T(8,128)(2,1)}, bf16[2,3,64,4096]{2,3,1,0:T(8,128)(2,1)S(1)}, u32[]{:S(2)}) copy-start(bf16[2,3,64,4096]{2,3,1,0:T(8,128)(2,1)S(1)} %broadcast_select_fusion) | copy-start | bytes 9437188
  10.7 75.9 %collective-permute-start = (bf16[1,2,3,64,256]{3,4,2,1,0:T(8,128)(2,1)S(1)}, bf16[1,2,3,64,256]{3,4,2,1,0:T(8,128)(2,1)}, u32[]{:S(2)}, u32[]{:S(2)}) collective-permute-start(bf16[1,2,3,64,256]{3,4,2,1,0:T(8,128)(2,1)S(1)} %bitcast.152), channel_id=1, source_target_pairs={{0,128},{1,129},{2,130},{3,131},{4,132},{5,133},{6,134},{7,135},{8... | collective-permute-start | bytes 589832 | tf_op jit(solution)/shard_map/ppermute | solution.py:18
  13.3 78.3 %collective-permute-start.1 = (bf16[1,2,3,64,256]{3,4,2,1,0:T(8,128)(2,1)S(1)}, bf16[1,2,3,64,256]{3,4,2,1,0:T(8,128)(2,1)}, u32[]{:S(2)}, u32[]{:S(2)}) collective-permute-start(bf16[1,2,3,64,256]{3,4,2,1,0:T(8,128)(2,1)S(1)} %bitcast.154), channel_id=1, source_target_pairs={{128,0},{129,1},{130,2},{131,3},{132,4},{133,5},{134,6},{135,7},{1... | collective-permute-start | bytes 589832 | tf_op jit(solution)/shard_map/ppermute | solution.py:19
  14.8 78.8 %collective-permute-start.2 = (bf16[1,2,3,64,256]{3,4,2,1,0:T(8,128)(2,1)S(1)}, bf16[1,2,3,64,256]{3,4,2,1,0:T(8,128)(2,1)}, u32[]{:S(2)}, u32[]{:S(2)}) collective-permute-start(bf16[1,2,3,64,256]{3,4,2,1,0:T(8,128)(2,1)S(1)} %bitcast.148), channel_id=1, source_target_pairs={{0,64},{1,65},{2,66},{3,67},{4,68},{5,69},{6,70},{7,71},{8,72},{9,... | collective-permute-start | bytes 589832 | tf_op jit(solution)/shard_map/ppermute | solution.py:18
  16.1 79.4 %collective-permute-start.3 = (bf16[1,2,3,64,256]{3,4,2,1,0:T(8,128)(2,1)S(1)}, bf16[1,2,3,64,256]{3,4,2,1,0:T(8,128)(2,1)}, u32[]{:S(2)}, u32[]{:S(2)}) collective-permute-start(bf16[1,2,3,64,256]{3,4,2,1,0:T(8,128)(2,1)S(1)} %bitcast.150), channel_id=1, source_target_pairs={{64,0},{65,1},{66,2},{67,3},{68,4},{69,5},{70,6},{71,7},{72,8},{73... | collective-permute-start | bytes 589832 | tf_op jit(solution)/shard_map/ppermute | solution.py:19
  24.9 72.5 %collective-permute-start.4 = (bf16[1,2,3,64,256]{3,4,2,1,0:T(8,128)(2,1)S(1)}, bf16[1,2,3,64,256]{3,4,2,1,0:T(8,128)(2,1)}, u32[]{:S(2)}, u32[]{:S(2)}) collective-permute-start(bf16[1,2,3,64,256]{3,4,2,1,0:T(8,128)(2,1)S(1)} %bitcast.146), channel_id=1, source_target_pairs={{0,1},{1,2},{2,3},{3,4},{4,5},{5,6},{6,7},{7,8},{8,9},{9,10},{10,1... | collective-permute-start | bytes 589832 | tf_op jit(solution)/shard_map/ppermute | solution.py:18
  46.6 8.6 %copy-start.2 = (s32[2,6]{1,0:T(2,128)S(1)}, s32[2,6]{1,0:T(2,128)}, u32[]{:S(2)}) copy-start(s32[2,6]{1,0:T(2,128)} %param.11) | copy-start | bytes 148
  46.6 8.7 %copy-start.5 = (s32[1,128]{1,0:T(1,128)S(1)}, s32[1,128]{1,0:T(1,128)}, u32[]{:S(2)}) copy-start(s32[1,128]{1,0:T(1,128)} %param.15) | copy-start | bytes 1540
  46.6 8.8 %copy-start.1 = (s32[512]{0:T(512)S(1)}, s32[512]{0:T(512)}, u32[]{:S(2)}) copy-start(s32[512]{0:T(512)} %param.12) | copy-start | bytes 6148
  46.6 10.1 %copy-start.3 = (f32[16]{0:T(128)S(1)}, f32[16]{0:T(128)}, u32[]{:S(2)}) copy-start(f32[16]{0:T(128)} %param.14) | copy-start | bytes 196
  46.6 10.1 %copy-start.4 = (f32[16]{0:T(128)S(1)}, f32[16]{0:T(128)}, u32[]{:S(2)}) copy-start(f32[16]{0:T(128)} %param.13) | copy-start | bytes 196
  86.6 13.8 %collective-permute-start.5 = (bf16[1,2,3,64,256]{3,4,2,1,0:T(8,128)(2,1)S(1)}, bf16[1,2,3,64,256]{3,4,2,1,0:T(8,128)(2,1)S(1)}, u32[]{:S(2)}, u32[]{:S(2)}) collective-permute-start(bf16[1,2,3,64,256]{3,4,2,1,0:T(8,128)(2,1)S(1)} %bitcast.156), channel_id=1, source_target_pairs={{1,0},{2,1},{3,2},{4,3},{5,4},{6,5},{7,6},{8,7},{9,8},{10,9},{11,1... | collective-permute-start | bytes 589832 | tf_op jit(solution)/shard_map/ppermute | solution.py:19

commit v2 on v0

v2 whole, which is shorter than its diff:
```python
import functools

import jax
import jax.numpy as jnp
from jax import lax
from jax.experimental import pallas as pl
from jax.experimental.pallas import tpu as pltpu
from jax.sharding import PartitionSpec as P

BX = 16
SLAB = 256
CELLS = 4096
NV = 64
ROWS = 128
PEERS = 64
LANES = 128
GROUP = 4
MESH = pl.DeviceIdType.MESH
F32 = jnp.float32
BF16 = jnp.bfloat16
TRANS = (((1,), (1,)), ((), ()))


def iota(shape, dim):
    return lax.broadcasted_iota(jnp.int32, shape, dim)


def picked(flag):
    return jnp.where(flag, 1.0, 0.0).astype(BF16)


def by_sub(first, second, shape):
    return jnp.where(iota(shape, len(shape) - 1) < NV, first, second)


def kernel(
    zvecs, counts, adjacency, mat_id, shear, ratio, owner,
    out,
    u, weave, select, faces, far, send1, recv1, send2, recv2,
    load_sem, face_send, face_recv, a2a_send, a2a_recv,
):
    gx, gy, gz = lax.axis_index("gx"), lax.axis_index("gy"), lax.axis_index("gz")
    device = (gx * 2 + gy) * PEERS + gz

    loads = []
    for c in range(3):
        for s in range(2):
            loads.append(
                pltpu.make_async_copy(
                    zvecs.at[s, c],
                    u.at[c, pl.ds(s * NV, NV), pl.ds(SLAB, CELLS)],
                    load_sem.at[c, s],
                )
            )
            loads[-1].start()

    barrier = pltpu.get_barrier_semaphore()
    pl.semaphore_signal(barrier, inc=1, device_id={"gx": 1 - gx}, device_id_type=MESH)
    pl.semaphore_signal(barrier, inc=1, device_id={"gy": 1 - gy}, device_id_type=MESH)

    def greet(k, carry):
        pl.semaphore_signal(
            barrier, inc=1, device_id={"gz": lax.rem(gz + k, PEERS)}, device_id_type=MESH
        )
        return carry

    lax.fori_loop(1, PEERS, greet, 0)

    col = iota((1, LANES), 1)
    base = (col // BX) * SLAB
    inner = col % BX
    targets = (base + (1 - gy) * 15 * BX + inner, base + inner * BX, base + inner * BX + 15)

    def fill(k, carry):
        row = iota((SLAB, LANES), 0) + k * SLAB
        for f in range(3):
            select[pl.ds(pl.multiple_of(k * SLAB, SLAB), SLAB), f * LANES : (f + 1) * LANES] = picked(
                row == targets[f]
            )
        return carry

    lax.fori_loop(0, 8, fill, 0)

    row = iota((SLAB, SLAB), 0)
    cell = iota((SLAB, SLAB), 1)
    zpos = cell % BX
    diag = jnp.where(row == cell, 2.0, 0.0)
    along_y = diag - jnp.where((row == cell + BX) | (row == cell - BX), 1.0, 0.0)
    along_z = diag - jnp.where(
        ((row == cell + 1) & (zpos < BX - 1)) | ((row == cell - 1) & (zpos > 0)), 1.0, 0.0
    )
    weave[:, 0:SLAB] = (along_y + along_z).astype(BF16)
    weave[:, SLAB : 2 * SLAB] = along_y.astype(BF16)
    weave[:, 2 * SLAB : 3 * SLAB] = along_z.astype(BF16)

    rows_of = iota((ROWS, 1), 0)
    used = jnp.where(rows_of < NV, counts[0], counts[1] + NV)
    keep = jnp.where(rows_of < used, 1.0, 0.0)

    zero_slab = jnp.zeros((ROWS, SLAB), BF16)
    near_x = (1 - gx) * 15 + 1
    for c in range(3):
        u[c, :, 0:SLAB] = zero_slab
        u[c, :, SLAB + CELLS : 2 * SLAB + CELLS] = zero_slab
        loads[2 * c].wait()
        loads[2 * c + 1].wait()
        for h in range(2):
            got = jnp.dot(
                u[c, :, SLAB + h * 2048 : SLAB + (h + 1) * 2048],
                select[...],
                preferred_element_type=F32,
            )
            got = (got * keep).astype(BF16)
            for f in range(3):
                faces[f + 1, c, :, h * LANES : (h + 1) * LANES] = got[:, f * LANES : (f + 1) * LANES]
        edge = u[c, :, pl.ds(pl.multiple_of(near_x * SLAB, SLAB), SLAB)].astype(F32)
        faces[0, c] = (edge * keep).astype(BF16)

    pl.semaphore_wait(barrier, PEERS + 1)
    moves = []
    for slot, source, target in (
        (1, 1, {"gy": 1 - gy}),
        (2, 3, {"gz": lax.rem(gz + 1, PEERS)}),
        (0, 0, {"gx": 1 - gx}),
    ):
        moves.append(
            pltpu.make_async_remote_copy(
                src_ref=faces.at[source],
                dst_ref=far.at[slot],
                send_sem=face_send.at[slot],
                recv_sem=face_recv.at[slot],
                device_id=target,
                device_id_type=MESH,
            )
        )
        moves[-1].start()

    own = [mat_id[device * 2 + s] for s in range(2)]
    own_shear = [shear[m] for m in own]
    own_ratio = [ratio[m] for m in own]
    by_row = rows_of < NV
    scale = jnp.where(by_row, own_shear[0], own_shear[1])
    extra = jnp.where(by_row, own_shear[0] * own_ratio[0], own_shear[1] * own_ratio[1])

    total = jnp.zeros((ROWS, ROWS), F32)
    for c in range(3):

        def group(g, total, c=c):
            start = pl.multiple_of(g * (GROUP * SLAB), GROUP * SLAB)
            slabs = [u[c, :, pl.ds(start + i * SLAB, SLAB)] for i in range(GROUP + 2)]
            stacked = jnp.concatenate(slabs[1:-1], axis=0)
            flat = jnp.dot(stacked, weave[:, 0:SLAB], preferred_element_type=F32)
            if c > 0:
                lone = jnp.dot(
                    stacked, weave[:, c * SLAB : (c + 1) * SLAB], preferred_element_type=F32
                )
            for i in range(GROUP):
                lower, here, upper = [slabs[i + k].astype(F32) for k in range(3)]
                along_x = 2.0 * here - upper - lower
                rest = flat[i * ROWS : (i + 1) * ROWS]
                special = along_x if c == 0 else lone[i * ROWS : (i + 1) * ROWS]
                applied = (scale * (along_x + rest) + extra * special).astype(BF16)
                total = total + lax.dot_general(
                    slabs[i + 1], applied, TRANS, preferred_element_type=F32
                )
            return total

        total = lax.fori_loop(0, BX // GROUP, group, total)

    shape = (NV, LANES)
    v_of = iota(shape, 0)
    w_of = iota(shape, 1)
    limit = by_sub(counts[0], counts[1], shape)
    inside = (v_of < limit) & (lax.rem(w_of, NV) < limit)
    block = by_sub(total[0:NV], total[NV:ROWS], shape)
    send1[pl.ds(0, NV, stride=8), :] = jnp.where(inside, block, 0.0)

    def couple(left, right, weights):
        result = None
        for c in range(3):
            full = lax.dot_general(left(c), right(c), TRANS, preferred_element_type=F32)
            result = weights[c] * full if result is None else result + weights[c] * full
        return result

    def matched(full, swap):
        turned = pltpu.roll(full, NV, 1)
        return by_sub(
            jnp.where(swap[0], turned[0:NV], full[0:NV]),
            jnp.where(swap[1], turned[NV:ROWS], full[NV:ROWS]),
            shape,
        )

    def pairing(slot, direction):
        swap, values = [], []
        for s in range(2):
            other = adjacency[s, slot]
            there = mat_id[jnp.maximum(other, 0)]
            there_shear, there_ratio = shear[there], ratio[there]
            other = jnp.full((1, LANES), other, jnp.int32)
            swap.append((other >= 0) & ((other & 1) != s))
            valid = jnp.where(other >= 0, -1.0, 0.0)
            line = []
            for c in range(3):
                unit = 1.0 if c == direction else 0.0
                product = (own_shear[s] * (1.0 + own_ratio[s] * unit)) * (
                    there_shear * (1.0 + there_ratio * unit)
                )
                line.append(valid * jnp.sqrt(jnp.full((1, LANES), product, F32)))
            values.append(line)
        return swap, values

    for order, (direction, slot, near, line) in enumerate(
        ((0, 1 - gx, 0, 1), (1, 3 - gy, 1, 2), (2, 4, 2, 3))
    ):
        swap, values = pairing(slot, direction)
        moves[(2, 0, 1)[order]].wait_recv()
        weights = [jnp.where(by_row, values[0][c], values[1][c]) for c in range(3)]
        full = couple(lambda c: faces[near, c], lambda c: far[direction, c], weights)
        send1[pl.ds(line, NV, stride=8), :] = matched(full, swap)
        if direction == 2:
            weights = [by_sub(values[0][c], values[1][c], (1, LANES)) for c in range(3)]
            full = couple(lambda c: far[2, c], lambda c: faces[2, c], weights)
            send1[pl.ds(4, NV, stride=8), :] = matched(full, swap)
    for move in moves:
        move.wait_send()

    def exchange(phase, source, target):
        def post(k, carry):
            peer = lax.rem(gz + k, PEERS)
            pltpu.make_async_remote_copy(
                src_ref=source.at[pl.ds(pl.multiple_of(peer * 8, 8), TILE)],
                dst_ref=target.at[pl.ds(pl.multiple_of(gz * 8, 8), TILE)],
                send_sem=a2a_send.at[phase],
                recv_sem=a2a_recv.at[phase],
                device_id={"gz": peer},
                device_id_type=MESH,
            ).start()
            return carry

        lax.fori_loop(1, PEERS, post, 0)
        mine = pl.ds(pl.multiple_of(gz * 8, 8), 8)
        target[mine, :] = source[mine, :]

    def arrive(phase, source, target):
        size = (PEERS - 1) * TILE
        whole = pltpu.make_async_remote_copy(
            src_ref=source.at[pl.ds(0, size)],
            dst_ref=target.at[pl.ds(0, size)],
            send_sem=a2a_send.at[phase],
            recv_sem=a2a_recv.at[phase],
            device_id={"gz": lax.rem(gz + 1, PEERS)},
            device_id_type=MESH,
        )
        whole.wait_recv()
        whole.wait_send()

    exchange(0, send1, recv1)

    line = iota((ROWS, ROWS), 0)
    spot = iota((ROWS, ROWS), 1)
    half = spot // NV
    holder = lax.rem(spot, NV)
    places = owner[...].astype(F32).astype(BF16)
    places = jnp.broadcast_to(places, (8, ROWS))
    want = (2 * lax.rem(line, NV) + line // NV).astype(F32)

    def moved(shift):
        sub = 2 * lax.rem(holder + (PEERS - shift), PEERS) + half
        place = jnp.dot(places, picked(line == sub), preferred_element_type=F32)
        hit = picked(place[0:1, :] == want)
        return jnp.concatenate([hit, hit, hit], axis=1)

    straight, shifted = moved(0), moved(1)
    arrive(0, send1, recv1)
    for b in range(5):
        chunk = recv1[pl.ds(b, PEERS, stride=8), :]
        turned = pltpu.roll(chunk, NV, 1)
        chunk = jnp.concatenate(
            [by_sub(chunk, turned, shape), by_sub(turned, chunk, shape)], axis=0
        )
        high = chunk.astype(BF16)
        left = chunk - high.astype(F32)
        middle = left.astype(BF16)
        low = (left - middle.astype(F32)).astype(BF16)
        full = jnp.dot(
            shifted if b == 4 else straight,
            jnp.concatenate([high, middle, low], axis=0),
            preferred_element_type=F32,
        )
        send2[pl.ds(b, PEERS, stride=8), :] = by_sub(full[0:NV], full[NV:ROWS], shape)

    exchange(1, send2, recv2)
    tile = (8, LANES)
    b_of = iota(tile, 0)
    x_at, y_at = 2 - gx, 4 - gy
    plain = (b_of == 0) | ((b_of == x_at) & (gx == 1))
    once = ((b_of == x_at) & (gx == 0)) | ((b_of == y_at) & (gy == 1))
    twice = ((b_of == y_at) & (gy == 0)) | (b_of > 4)
    arrive(1, send2, recv2)

    def place(m, carry):
        pair = [recv2[pl.ds(pl.multiple_of((2 * m + i) * 8, 8), 8), :] for i in range(2)]
        turned = [pltpu.roll(t, NV, 1) for t in pair]
        for p, value in enumerate(
            (by_sub(pair[0], turned[1], tile), by_sub(turned[0], pair[1], tile))
        ):
            value = jnp.where(
                plain,
                value,
                jnp.where(
                    once,
                    pltpu.roll(value, 1, 0),
                    jnp.where(twice, pltpu.roll(value, 2, 0), 0.0),
                ),
            )
            out[p, :, pl.ds(pl.multiple_of(m * LANES, LANES), LANES)] = value[0:7]
        return carry

    lax.fori_loop(0, CELLS // LANES, place, 0, unroll=4)


TILE = 5


def per_device(zvecs, counts, adjacency, mat_id, shear, ratio, owner_map):
    smem = pl.BlockSpec(memory_space=pltpu.SMEM)
    vmem = pl.BlockSpec(memory_space=pltpu.VMEM)
    rows = pl.pallas_call(
        kernel,
        out_shape=jax.ShapeDtypeStruct((2, 7, CELLS), F32),
        in_specs=[pl.BlockSpec(memory_space=pl.ANY), smem, smem, smem, smem, smem, vmem],
        out_specs=vmem,
        scratch_shapes=[
            pltpu.VMEM((3, ROWS, CELLS + 2 * SLAB), BF16),
            pltpu.VMEM((SLAB, 3 * SLAB), BF16),
            pltpu.VMEM((8 * SLAB, 3 * LANES), BF16),
            pltpu.VMEM((4, 3, ROWS, SLAB), BF16),
            pltpu.VMEM((3, 3, ROWS, SLAB), BF16),
            pltpu.VMEM((PEERS * 8, LANES), F32),
            pltpu.VMEM((PEERS * 8, LANES), F32),
            pltpu.VMEM((PEERS * 8, LANES), F32),
            pltpu.VMEM((PEERS * 8, LANES), F32),
            pltpu.SemaphoreType.DMA((3, 2)),
            pltpu.SemaphoreType.DMA((3,)),
            pltpu.SemaphoreType.DMA((3,)),
            pltpu.SemaphoreType.DMA((2,)),
            pltpu.SemaphoreType.DMA((2,)),
        ],
        compiler_params=pltpu.CompilerParams(collective_id=0, has_side_effects=True),
        name="assemble",
    )(zvecs, counts, adjacency, mat_id, shear, ratio, owner_map)
    return rows[None]


def solution(mesh):
    placed = (
        P(("gx", "gy", "gz"), None, None, None),
        P(("gx", "gy", "gz")),
        P(("gx", "gy", "gz"), None),
        P(),
        P(),
        P(),
        P(("gx", "gy"), None),
    )
    return jax.shard_map(
        per_device,
        mesh=mesh,
        in_specs=placed,
        out_specs=P(("gx", "gy"), "gz", None, None),
        check_vma=False,
    )
```

time: 477 us -> 41.6 us (0.09)
  blocking collectives: 335 us -> 0 us
  local copies, waits for them, and re-layouts: 79.2 us -> 1.82 us
  Pallas kernels: 0 us -> 39.6 us
  matrix products: 32 us -> 0 us
  starting transfers between devices: 16.8 us -> 0 us
  other arithmetic: 10.8 us -> 0 us
    all_to_all x1 -> x0, blocking collectives: 335 us -> none  [per_device(): lax.all_to_all(send, 'gz', split_axis=0, concat_axis=0, tiled=True)]
    pallas_call x0 -> x1, Pallas kernels: none -> 39.6 us  [per_device(): pl.pallas_call(kernel, out_shape=jax.ShapeDtypeStruct((2, 7, CELLS), F32)...]
    dot_general x7 -> x0, matrix products: 32 us -> none  [the longest x1 29.3 us: per_device(): jnp.einsum('scvx,scwx->svw', masked, applied, preferred_element_type=jnp....]
    slice x8 -> x0, local copies, waits for them, and re-layouts: 28.6 us -> none  [the longest x3 26.3 us: stencil(): upper = jnp.pad(plain[..., stride:], lead + [(0, stride)])]
    scatter x2 -> x0, local copies, waits for them, and re-layouts: 23.9 us -> none  [per_device(): send = send.at[places // subs, places % subs].set(rows)]
    ppermute x6 -> x0, starting transfers between devices: 16.8 us -> none  [the longest x3 9.39 us: extended(): after = lax.ppermute(initial, axis, down)]
    gather x9 -> x0, local copies, waits for them, and re-layouts: 9.83 us -> none  [the longest x3 4.58 us: per_device(): below = jnp.take(padded[0], local[:, 2 * direction], axis=0)]
    broadcast_in_dim x3 -> x1, local copies, waits for them, and re-layouts: 8.77 us -> 1.82 us  [per_device(): return rows[None]]
  transfers between devices with their start and end apart: 6 -> 0, of which waited for: 0 -> 0; matrix products, arithmetic and copies ran while one was open for 14% -> 0% of each run, Pallas kernels for 0% -> 0%
where the time goes in v2:
time: 41.6 us; the launch traced here: 41.4 us
  Pallas kernels  39.6 us (95%)
  local copies, waits for them, and re-layouts  1.82 us (4%)
    pallas_call x1, Pallas kernels, per_device(): pl.pallas_call(kernel, out_shape=jax.ShapeDtypeStruct((2, 7, CELLS), F32)...  39.6 us
    broadcast_in_dim x1, local copies, waits for them, and re-layouts, per_device(): return rows[None]  1.82 us

profile of v2, /device:TPU:4, one launch (start us, length us, event | category | flops | bytes accessed | tf_op | source)
XLA Modules:
  0.0 41.4 jit_solution(2832540863199677829)
XLA Ops:
  0.0 39.6 %assemble.1 = f32[2,7,4096]{2,1,0:T(8,128)} custom-call(bf16[2,3,64,4096]{3,2,1,0:T(8,128)(2,1)} %zvecs.1, s32[2]{0:T(128)} %counts.1, s32[2,6]{1,0:T(2,128)} %adjacency.1, s32[512]{0:T(512)} %mat_id.1, f32[16]{0:T(128)} %shear.1, f32[16]{0:T(128)} %ratio.1, s32[1,128]{1,0:T(1,128)} %owner.1), custom_call_target="tpu_custom_call" | custom-call | tf_op jit(solution)/shard_map/assemble/pallas_call | solution.py:328
  39.6 1.8 %copy.8 = f32[1,2,7,4096]{3,1,2,0:T(2,128)} copy(f32[1,2,7,4096]{3,2,1,0:T(8,128)} %bitcast.1) | data formatting | bytes 458752 | tf_op jit(solution)/shard_map/broadcast_in_dim | solution.py:352

commit v3 on v2

--- a/solution.py
+++ b/solution.py
@@ -36,8 +36,8 @@
 def kernel(
     zvecs, counts, adjacency, mat_id, shear, ratio, owner,
     out,
-    u, weave, select, faces, far, send1, recv1, send2, recv2,
-    load_sem, face_send, face_recv, a2a_send, a2a_recv,
+    u, weave, select, near, far, near_y, far_y, back_out, back_in, send1, recv1, send2, recv2,
+    load_sem, face_send, face_recv, back_sem, a2a_send, a2a_recv, ring_sem,
 ):
     gx, gy, gz = lax.axis_index("gx"), lax.axis_index("gy"), lax.axis_index("gz")
     device = (gx * 2 + gy) * PEERS + gz
@@ -58,13 +58,27 @@
     pl.semaphore_signal(barrier, inc=1, device_id={"gx": 1 - gx}, device_id_type=MESH)
     pl.semaphore_signal(barrier, inc=1, device_id={"gy": 1 - gy}, device_id_type=MESH)
 
-    def greet(k, carry):
-        pl.semaphore_signal(
-            barrier, inc=1, device_id={"gz": lax.rem(gz + k, PEERS)}, device_id_type=MESH
-        )
-        return carry
-
-    lax.fori_loop(1, PEERS, greet, 0)
+    plane, spot = gz // 8, lax.rem(gz, 8)
+    above = lax.rem(plane + 1, 8) * 8 + spot
+    below = lax.rem(plane + 7, 8) * 8 + spot
+    for peer in [lax.rem(gz + 1, PEERS), lax.rem(gz + PEERS - 1, PEERS), above, below] + [
+        plane * 8 + lax.rem(spot + k, 8) for k in range(1, 8)
+    ]:
+        pl.semaphore_signal(barrier, inc=1, device_id={"gz": peer}, device_id_type=MESH)
+
+    def pass_on(step):
+        if step > 0:
+            pl.semaphore_wait(ring_sem.at[0], 1)
+        if step < 4:
+            pl.semaphore_signal(
+                ring_sem.at[0], inc=1, device_id={"gz": above}, device_id_type=MESH
+            )
+        if 0 < step < 4:
+            pl.semaphore_wait(ring_sem.at[1], 1)
+        if step < 3:
+            pl.semaphore_signal(
+                ring_sem.at[1], inc=1, device_id={"gz": below}, device_id_type=MESH
+            )
 
     col = iota((1, LANES), 1)
     base = (col // BX) * SLAB
@@ -97,43 +111,53 @@
     used = jnp.where(rows_of < NV, counts[0], counts[1] + NV)
     keep = jnp.where(rows_of < used, 1.0, 0.0)
 
+    swapped = jnp.full((1, SLAB), adjacency[0, 3 - gy] & 1, jnp.int32)
+    keep_last = (swapped + (1 - gy)) > 0
+
     zero_slab = jnp.zeros((ROWS, SLAB), BF16)
     near_x = (1 - gx) * 15 + 1
+    moves = [[], [], []]
     for c in range(3):
         u[c, :, 0:SLAB] = zero_slab
         u[c, :, SLAB + CELLS : 2 * SLAB + CELLS] = zero_slab
         loads[2 * c].wait()
         loads[2 * c + 1].wait()
+        parts = []
         for h in range(2):
             got = jnp.dot(
                 u[c, :, SLAB + h * 2048 : SLAB + (h + 1) * 2048],
                 select[...],
                 preferred_element_type=F32,
             )
-            got = (got * keep).astype(BF16)
-            for f in range(3):
-                faces[f + 1, c, :, h * LANES : (h + 1) * LANES] = got[:, f * LANES : (f + 1) * LANES]
+            parts.append(got * keep)
+        layers = [
+            jnp.concatenate([p[:, f * LANES : (f + 1) * LANES] for p in parts], axis=1)
+            for f in range(3)
+        ]
+        near_y[0, c] = jnp.where(keep_last, layers[0][NV:ROWS], layers[0][0:NV]).astype(BF16)
+        near_y[1, c] = jnp.where(keep_last, layers[0][0:NV], layers[0][NV:ROWS]).astype(BF16)
+        near[1, c] = layers[1].astype(BF16)
+        near[2, c] = layers[2].astype(BF16)
         edge = u[c, :, pl.ds(pl.multiple_of(near_x * SLAB, SLAB), SLAB)].astype(F32)
-        faces[0, c] = (edge * keep).astype(BF16)
-
-    pl.semaphore_wait(barrier, PEERS + 1)
-    moves = []
-    for slot, source, target in (
-        (1, 1, {"gy": 1 - gy}),
-        (2, 3, {"gz": lax.rem(gz + 1, PEERS)}),
-        (0, 0, {"gx": 1 - gx}),
-    ):
-        moves.append(
-            pltpu.make_async_remote_copy(
-                src_ref=faces.at[source],
-                dst_ref=far.at[slot],
-                send_sem=face_send.at[slot],
-                recv_sem=face_recv.at[slot],
+        near[0, c] = (edge * keep).astype(BF16)
+        if c == 0:
+            pl.semaphore_wait(barrier, 13)
+            pass_on(0)
+        for slot, source, landing, target in (
+            (1, near_y.at[1, c], far_y.at[c], {"gy": 1 - gy}),
+            (2, near.at[2, c], far.at[1, c], {"gz": lax.rem(gz + 1, PEERS)}),
+            (0, near.at[0, c], far.at[0, c], {"gx": 1 - gx}),
+        ):
+            move = pltpu.make_async_remote_copy(
+                src_ref=source,
+                dst_ref=landing,
+                send_sem=face_send.at[slot, c],
+                recv_sem=face_recv.at[slot, c],
                 device_id=target,
                 device_id_type=MESH,
             )
-        )
-        moves[-1].start()
+            move.start()
+            moves[slot].append(move)
 
     own = [mat_id[device * 2 + s] for s in range(2)]
     own_shear = [shear[m] for m in own]
@@ -142,10 +166,8 @@
     scale = jnp.where(by_row, own_shear[0], own_shear[1])
     extra = jnp.where(by_row, own_shear[0] * own_ratio[0], own_shear[1] * own_ratio[1])
 
-    total = jnp.zeros((ROWS, ROWS), F32)
-    for c in range(3):
-
-        def group(g, total, c=c):
+    def stencil(c, total):
+        def group(g, total):
             start = pl.multiple_of(g * (GROUP * SLAB), GROUP * SLAB)
             slabs = [u[c, :, pl.ds(start + i * SLAB, SLAB)] for i in range(GROUP + 2)]
             stacked = jnp.concatenate(slabs[1:-1], axis=0)
@@ -165,15 +187,9 @@
                 )
             return total
 
-        total = lax.fori_loop(0, BX // GROUP, group, total)
+        return lax.fori_loop(0, BX // GROUP, group, total)
 
     shape = (NV, LANES)
-    v_of = iota(shape, 0)
-    w_of = iota(shape, 1)
-    limit = by_sub(counts[0], counts[1], shape)
-    inside = (v_of < limit) & (lax.rem(w_of, NV) < limit)
-    block = by_sub(total[0:NV], total[NV:ROWS], shape)
-    send1[pl.ds(0, NV, stride=8), :] = jnp.where(inside, block, 0.0)
 
     def couple(left, right, weights):
         result = None
@@ -209,24 +225,72 @@
             values.append(line)
         return swap, values
 
-    for order, (direction, slot, near, line) in enumerate(
-        ((0, 1 - gx, 0, 1), (1, 3 - gy, 1, 2), (2, 4, 2, 3))
-    ):
-        swap, values = pairing(slot, direction)
-        moves[(2, 0, 1)[order]].wait_recv()
-        weights = [jnp.where(by_row, values[0][c], values[1][c]) for c in range(3)]
-        full = couple(lambda c: faces[near, c], lambda c: far[direction, c], weights)
-        send1[pl.ds(line, NV, stride=8), :] = matched(full, swap)
-        if direction == 2:
-            weights = [by_sub(values[0][c], values[1][c], (1, LANES)) for c in range(3)]
-            full = couple(lambda c: far[2, c], lambda c: faces[2, c], weights)
-            send1[pl.ds(4, NV, stride=8), :] = matched(full, swap)
-    for move in moves:
-        move.wait_send()
+    pass_on(1)
+    total = stencil(0, jnp.zeros((ROWS, ROWS), F32))
+    pass_on(2)
+    total = stencil(1, total)
+    pass_on(3)
+
+    _, values = pairing(3 - gy, 1)
+    keep_here = keep_last[:, 0:LANES]
+    weights = [jnp.where(keep_here, values[1][c], values[0][c]) for c in range(3)]
+    for move in moves[1]:
+        move.wait_recv()
+    twice = lambda ref, c: jnp.concatenate([ref[c], ref[c]], axis=0)
+    kept = couple(lambda c: near_y[0, c], lambda c: twice(far_y, c), weights)
+    other = couple(lambda c: far_y[c], lambda c: twice(near_y.at[0], c), weights)
+    back_out[...] = by_sub(other[0 : NV // 2], other[NV // 2 : NV], (NV // 2, LANES))
+    back = pltpu.make_async_remote_copy(
+        src_ref=back_out,
+        dst_ref=back_in,
+        send_sem=back_sem.at[0],
+        recv_sem=back_sem.at[1],
+        device_id={"gy": 1 - gy},
+        device_id_type=MESH,
+    )
+    back.start()
+
+    total = stencil(2, total)
+    v_of = iota(shape, 0)
+    w_of = iota(shape, 1)
+    limit = by_sub(counts[0], counts[1], shape)
+    inside = (v_of < limit) & (lax.rem(w_of, NV) < limit)
+    block = by_sub(total[0:NV], total[NV:ROWS], shape)
+    send1[pl.ds(0, NV, stride=8), :] = jnp.where(inside, block, 0.0)
+
+    swap, values = pairing(1 - gx, 0)
+    for move in moves[0]:
+        move.wait_recv()
+    weights = [jnp.where(by_row, values[0][c], values[1][c]) for c in range(3)]
+    full = couple(lambda c: near[0, c], lambda c: far[0, c], weights)
+    send1[pl.ds(1, NV, stride=8), :] = matched(full, swap)
+
+    back.wait_recv()
+    packed = back_in[...]
+    turned = pltpu.roll(packed, NV, 1)
+    given = jnp.concatenate(
+        [by_sub(packed, turned, packed.shape), by_sub(turned, packed, packed.shape)], axis=0
+    )
+    send1[pl.ds(2, NV, stride=8), :] = by_sub(
+        jnp.where(keep_here, given, kept), jnp.where(keep_here, kept, given), shape
+    )
+
+    swap, values = pairing(4, 2)
+    for move in moves[2]:
+        move.wait_recv()
+    weights = [jnp.where(by_row, values[0][c], values[1][c]) for c in range(3)]
+    full = couple(lambda c: near[1, c], lambda c: far[1, c], weights)
+    send1[pl.ds(3, NV, stride=8), :] = matched(full, swap)
+    weights = [by_sub(values[0][c], values[1][c], (1, LANES)) for c in range(3)]
+    full = couple(lambda c: far[1, c], lambda c: near[1, c], weights)
+    send1[pl.ds(4, NV, stride=8), :] = matched(full, swap)
 
     def exchange(phase, source, target):
         def post(k, carry):
-            peer = lax.rem(gz + k, PEERS)
+            ring = k // 8
+            step = (ring + 1) // 2
+            ring = PEERS // 16 + step * (2 * lax.rem(ring, 2) - 1)
+            peer = lax.rem(gz // 8 + ring, 8) * 8 + lax.rem(gz + k + 1, 8)
             pltpu.make_async_remote_copy(
                 src_ref=source.at[pl.ds(pl.multiple_of(peer * 8, 8), TILE)],
                 dst_ref=target.at[pl.ds(pl.multiple_of(gz * 8, 8), TILE)],
@@ -237,13 +301,13 @@
             ).start()
             return carry
 
-        lax.fori_loop(1, PEERS, post, 0)
+        lax.fori_loop(0, PEERS - 1, post, 0)
         mine = pl.ds(pl.multiple_of(gz * 8, 8), 8)
         target[mine, :] = source[mine, :]
 
-    def arrive(phase, source, target):
+    def whole(phase, source, target):
         size = (PEERS - 1) * TILE
-        whole = pltpu.make_async_remote_copy(
+        return pltpu.make_async_remote_copy(
             src_ref=source.at[pl.ds(0, size)],
             dst_ref=target.at[pl.ds(0, size)],
             send_sem=a2a_send.at[phase],
@@ -251,9 +315,8 @@
             device_id={"gz": lax.rem(gz + 1, PEERS)},
             device_id_type=MESH,
         )
-        whole.wait_recv()
-        whole.wait_send()
-
+
+    pass_on(4)
     exchange(0, send1, recv1)
 
     line = iota((ROWS, ROWS), 0)
@@ -271,7 +334,7 @@
         return jnp.concatenate([hit, hit, hit], axis=1)
 
     straight, shifted = moved(0), moved(1)
-    arrive(0, send1, recv1)
+    whole(0, send1, recv1).wait_recv()
     for b in range(5):
         chunk = recv1[pl.ds(b, PEERS, stride=8), :]
         turned = pltpu.roll(chunk, NV, 1)
@@ -296,7 +359,7 @@
     plain = (b_of == 0) | ((b_of == x_at) & (gx == 1))
     once = ((b_of == x_at) & (gx == 0)) | ((b_of == y_at) & (gy == 1))
     twice = ((b_of == y_at) & (gy == 0)) | (b_of > 4)
-    arrive(1, send2, recv2)
+    whole(1, send2, recv2).wait_recv()
 
     def place(m, carry):
         pair = [recv2[pl.ds(pl.multiple_of((2 * m + i) * 8, 8), 8), :] for i in range(2)]
@@ -313,10 +376,12 @@
                     jnp.where(twice, pltpu.roll(value, 2, 0), 0.0),
                 ),
             )
-            out[p, :, pl.ds(pl.multiple_of(m * LANES, LANES), LANES)] = value[0:7]
+            out[:, p, pl.ds(pl.multiple_of(m * LANES, LANES), LANES)] = value[0:7]
         return carry
 
     lax.fori_loop(0, CELLS // LANES, place, 0, unroll=4)
+    for move in moves[0] + moves[1] + moves[2] + [back, whole(0, send1, recv1), whole(1, send2, recv2)]:
+        move.wait_send()
 
 
 TILE = 5
@@ -327,29 +392,35 @@
     vmem = pl.BlockSpec(memory_space=pltpu.VMEM)
     rows = pl.pallas_call(
         kernel,
-        out_shape=jax.ShapeDtypeStruct((2, 7, CELLS), F32),
+        out_shape=jax.ShapeDtypeStruct((7, 2, CELLS), F32),
         in_specs=[pl.BlockSpec(memory_space=pl.ANY), smem, smem, smem, smem, smem, vmem],
         out_specs=vmem,
         scratch_shapes=[
             pltpu.VMEM((3, ROWS, CELLS + 2 * SLAB), BF16),
             pltpu.VMEM((SLAB, 3 * SLAB), BF16),
             pltpu.VMEM((8 * SLAB, 3 * LANES), BF16),
-            pltpu.VMEM((4, 3, ROWS, SLAB), BF16),
             pltpu.VMEM((3, 3, ROWS, SLAB), BF16),
+            pltpu.VMEM((2, 3, ROWS, SLAB), BF16),
+            pltpu.VMEM((2, 3, NV, SLAB), BF16),
+            pltpu.VMEM((3, NV, SLAB), BF16),
+            pltpu.VMEM((NV // 2, LANES), F32),
+            pltpu.VMEM((NV // 2, LANES), F32),
             pltpu.VMEM((PEERS * 8, LANES), F32),
             pltpu.VMEM((PEERS * 8, LANES), F32),
             pltpu.VMEM((PEERS * 8, LANES), F32),
             pltpu.VMEM((PEERS * 8, LANES), F32),
             pltpu.SemaphoreType.DMA((3, 2)),
-            pltpu.SemaphoreType.DMA((3,)),
-            pltpu.SemaphoreType.DMA((3,)),
+            pltpu.SemaphoreType.DMA((3, 3)),
+            pltpu.SemaphoreType.DMA((3, 3)),
             pltpu.SemaphoreType.DMA((2,)),
             pltpu.SemaphoreType.DMA((2,)),
+            pltpu.SemaphoreType.DMA((2,)),
+            pltpu.SemaphoreType.REGULAR((2,)),
         ],
         compiler_params=pltpu.CompilerParams(collective_id=0, has_side_effects=True),
         name="assemble",
     )(zvecs, counts, adjacency, mat_id, shear, ratio, owner_map)
-    return rows[None]
+    return jnp.transpose(rows, (1, 0, 2))[None]
 
 
 def solution(mesh):

time: 41.6 us -> 38.5 us (0.925)
  Pallas kernels: 39.6 us -> 36.7 us
    pallas_call x1, Pallas kernels: 39.6 us -> 36.7 us  [per_device(): pl.pallas_call(kernel, out_shape=jax.ShapeDtypeStruct((7, 2, CELLS), F32)...]
    broadcast_in_dim x1 -> x0, local copies, waits for them, and re-layouts: 1.82 us -> none  [per_device(): return rows[None]]
    unnamed x0 -> x1, local copies, waits for them, and re-layouts: none -> 1.64 us
where the time goes in v3:
time: 38.5 us; the launch traced here: 38.4 us
  Pallas kernels  36.7 us (95%)
  local copies, waits for them, and re-layouts  1.64 us (4%)
    pallas_call x1, Pallas kernels, per_device(): pl.pallas_call(kernel, out_shape=jax.ShapeDtypeStruct((7, 2, CELLS), F32)...  36.7 us
    unnamed x1, local copies, waits for them, and re-layouts  1.64 us

profile of v3, /device:TPU:4, one launch (start us, length us, event | category | flops | bytes accessed | tf_op | source)
XLA Modules:
  0.0 38.4 jit_solution(8967562276053318299)
XLA Ops:
  0.0 36.7 %assemble.1 = f32[7,2,4096]{2,1,0:T(2,128)} custom-call(bf16[2,3,64,4096]{3,2,1,0:T(8,128)(2,1)} %zvecs.1, s32[2]{0:T(128)} %counts.1, s32[2,6]{1,0:T(2,128)} %adjacency.1, s32[512]{0:T(512)} %mat_id.1, f32[16]{0:T(128)} %shear.1, f32[16]{0:T(128)} %ratio.1, s32[1,128]{1,0:T(1,128)} %owner.1), custom_call_target="tpu_custom_call" | custom-call | tf_op jit(solution)/shard_map/assemble/pallas_call | solution.py:393
  36.7 1.6 %copy.9 = f32[1,2,7,4096]{3,1,2,0:T(2,128)} copy(f32[1,2,7,4096]{3,1,2,0:T(2,128)} %bitcast.3) | data formatting | bytes 458752

commit v4 on v3

--- a/solution.py
+++ b/solution.py
@@ -15,6 +15,8 @@
 PEERS = 64
 LANES = 128
 GROUP = 4
+UNROLL = 1
+UNROLL_POST = 1
 MESH = pl.DeviceIdType.MESH
 F32 = jnp.float32
 BF16 = jnp.bfloat16
@@ -41,6 +43,16 @@
 ):
     gx, gy, gz = lax.axis_index("gx"), lax.axis_index("gy"), lax.axis_index("gz")
     device = (gx * 2 + gy) * PEERS + gz
+
+    barrier = pltpu.get_barrier_semaphore()
+    pl.semaphore_signal(barrier, inc=1, device_id={"gx": 1 - gx}, device_id_type=MESH)
+    pl.semaphore_signal(barrier, inc=1, device_id={"gy": 1 - gy}, device_id_type=MESH)
+
+    plane, spot = gz // 8, gz & 7
+    after, before = (gz + 1) & (PEERS - 1), (gz + PEERS - 1) & (PEERS - 1)
+    above, below = (gz + 8) & (PEERS - 1), (gz + PEERS - 8) & (PEERS - 1)
+    for peer in [after, before, above, below] + [plane * 8 + (spot ^ k) for k in range(1, 8)]:
+        pl.semaphore_signal(barrier, inc=1, device_id={"gz": peer}, device_id_type=MESH)
 
     loads = []
     for c in range(3):
@@ -53,18 +65,6 @@
                 )
             )
             loads[-1].start()
-
-    barrier = pltpu.get_barrier_semaphore()
-    pl.semaphore_signal(barrier, inc=1, device_id={"gx": 1 - gx}, device_id_type=MESH)
-    pl.semaphore_signal(barrier, inc=1, device_id={"gy": 1 - gy}, device_id_type=MESH)
-
-    plane, spot = gz // 8, lax.rem(gz, 8)
-    above = lax.rem(plane + 1, 8) * 8 + spot
-    below = lax.rem(plane + 7, 8) * 8 + spot
-    for peer in [lax.rem(gz + 1, PEERS), lax.rem(gz + PEERS - 1, PEERS), above, below] + [
-        plane * 8 + lax.rem(spot + k, 8) for k in range(1, 8)
-    ]:
-        pl.semaphore_signal(barrier, inc=1, device_id={"gz": peer}, device_id_type=MESH)
 
     def pass_on(step):
         if step > 0:
@@ -80,32 +80,17 @@
                 ring_sem.at[1], inc=1, device_id={"gz": below}, device_id_type=MESH
             )
 
-    col = iota((1, LANES), 1)
-    base = (col // BX) * SLAB
-    inner = col % BX
-    targets = (base + (1 - gy) * 15 * BX + inner, base + inner * BX, base + inner * BX + 15)
-
-    def fill(k, carry):
-        row = iota((SLAB, LANES), 0) + k * SLAB
+    inner = iota((SLAB, LANES), 1) % BX
+    cell = iota((SLAB, LANES), 0)
+    patterns = [
+        picked(cell == target)
+        for target in ((1 - gy) * 15 * BX + inner, inner * BX + 15, inner * BX)
+    ]
+    lane_slab = iota((1, LANES), 1) // BX
+    for k in range(8):
+        part = picked(lane_slab == k)
         for f in range(3):
-            select[pl.ds(pl.multiple_of(k * SLAB, SLAB), SLAB), f * LANES : (f + 1) * LANES] = picked(
-                row == targets[f]
-            )
-        return carry
-
-    lax.fori_loop(0, 8, fill, 0)
-
-    row = iota((SLAB, SLAB), 0)
-    cell = iota((SLAB, SLAB), 1)
-    zpos = cell % BX
-    diag = jnp.where(row == cell, 2.0, 0.0)
-    along_y = diag - jnp.where((row == cell + BX) | (row == cell - BX), 1.0, 0.0)
-    along_z = diag - jnp.where(
-        ((row == cell + 1) & (zpos < BX - 1)) | ((row == cell - 1) & (zpos > 0)), 1.0, 0.0
-    )
-    weave[:, 0:SLAB] = (along_y + along_z).astype(BF16)
-    weave[:, SLAB : 2 * SLAB] = along_y.astype(BF16)
-    weave[:, 2 * SLAB : 3 * SLAB] = along_z.astype(BF16)
+            select[k * SLAB : (k + 1) * SLAB, f * LANES : (f + 1) * LANES] = patterns[f] * part
 
     rows_of = iota((ROWS, 1), 0)
     used = jnp.where(rows_of < NV, counts[0], counts[1] + NV)
@@ -113,6 +98,33 @@
 
     swapped = jnp.full((1, SLAB), adjacency[0, 3 - gy] & 1, jnp.int32)
     keep_last = (swapped + (1 - gy)) > 0
+
+    def layers(c, first, last):
+        halves = [u[c, :, SLAB + h * 2048 : SLAB + (h + 1) * 2048] for h in range(2)]
+        got = jnp.dot(
+            jnp.concatenate(halves, axis=0),
+            select[:, first * LANES : last * LANES],
+            preferred_element_type=F32,
+        )
+        return [
+            jnp.concatenate(
+                [got[h * ROWS : (h + 1) * ROWS, f * LANES : (f + 1) * LANES] * keep for h in range(2)],
+                axis=1,
+            )
+            for f in range(last - first)
+        ]
+
+    def send(slot, c, source, landing, target):
+        move = pltpu.make_async_remote_copy(
+            src_ref=source,
+            dst_ref=landing,
+            send_sem=face_send.at[slot, c],
+            recv_sem=face_recv.at[slot, c],
+            device_id=target,
+            device_id_type=MESH,
+        )
+        move.start()
+        moves[slot].append(move)
 
     zero_slab = jnp.zeros((ROWS, SLAB), BF16)
     near_x = (1 - gx) * 15 + 1
@@ -122,42 +134,34 @@
         u[c, :, SLAB + CELLS : 2 * SLAB + CELLS] = zero_slab
         loads[2 * c].wait()
         loads[2 * c + 1].wait()
-        parts = []
-        for h in range(2):
-            got = jnp.dot(
-                u[c, :, SLAB + h * 2048 : SLAB + (h + 1) * 2048],
-                select[...],
-                preferred_element_type=F32,
-            )
-            parts.append(got * keep)
-        layers = [
-            jnp.concatenate([p[:, f * LANES : (f + 1) * LANES] for p in parts], axis=1)
-            for f in range(3)
-        ]
-        near_y[0, c] = jnp.where(keep_last, layers[0][NV:ROWS], layers[0][0:NV]).astype(BF16)
-        near_y[1, c] = jnp.where(keep_last, layers[0][0:NV], layers[0][NV:ROWS]).astype(BF16)
-        near[1, c] = layers[1].astype(BF16)
-        near[2, c] = layers[2].astype(BF16)
+        layer_y, layer_z, layer_low = layers(c, 0, 3)
+        near[1, c] = layer_low.astype(BF16)
+        near_y[0, c] = jnp.where(keep_last, layer_y[NV:ROWS], layer_y[0:NV]).astype(BF16)
+        near_y[1, c] = jnp.where(keep_last, layer_y[0:NV], layer_y[NV:ROWS]).astype(BF16)
+        near[2, c] = layer_z.astype(BF16)
         edge = u[c, :, pl.ds(pl.multiple_of(near_x * SLAB, SLAB), SLAB)].astype(F32)
         near[0, c] = (edge * keep).astype(BF16)
         if c == 0:
             pl.semaphore_wait(barrier, 13)
             pass_on(0)
-        for slot, source, landing, target in (
-            (1, near_y.at[1, c], far_y.at[c], {"gy": 1 - gy}),
-            (2, near.at[2, c], far.at[1, c], {"gz": lax.rem(gz + 1, PEERS)}),
-            (0, near.at[0, c], far.at[0, c], {"gx": 1 - gx}),
-        ):
-            move = pltpu.make_async_remote_copy(
-                src_ref=source,
-                dst_ref=landing,
-                send_sem=face_send.at[slot, c],
-                recv_sem=face_recv.at[slot, c],
-                device_id=target,
-                device_id_type=MESH,
-            )
-            move.start()
-            moves[slot].append(move)
+        send(1, c, near_y.at[1, c], far_y.at[c], {"gy": 1 - gy})
+    for c in range(3):
+        send(2, c, near.at[2, c], far.at[1, c], {"gz": after})
+    for c in range(3):
+        send(0, c, near.at[0, c], far.at[0, c], {"gx": 1 - gx})
+
+    row = iota((SLAB, SLAB), 0)
+    cell = iota((SLAB, SLAB), 1)
+    zpos = cell % BX
+    diag = jnp.where(row == cell, 2.0, 0.0)
+    along_y = diag - jnp.where((row == cell + BX) | (row == cell - BX), 1.0, 0.0)
+    along_z = diag - jnp.where(
+        ((row == cell + 1) & (zpos < BX - 1)) | ((row == cell - 1) & (zpos > 0)), 1.0, 0.0
+    )
+    weave[:, 0:SLAB] = (along_y + along_z).astype(BF16)
+    weave[:, 3 * SLAB : 4 * SLAB] = (along_y + along_z + diag).astype(BF16)
+    weave[:, SLAB : 2 * SLAB] = along_y.astype(BF16)
+    weave[:, 2 * SLAB : 3 * SLAB] = along_z.astype(BF16)
 
     own = [mat_id[device * 2 + s] for s in range(2)]
     own_shear = [shear[m] for m in own]
@@ -166,28 +170,36 @@
     scale = jnp.where(by_row, own_shear[0], own_shear[1])
     extra = jnp.where(by_row, own_shear[0] * own_ratio[0], own_shear[1] * own_ratio[1])
 
+    both = scale + extra
+
     def stencil(c, total):
+        first = 0 if c == 0 else 3 * SLAB
+
         def group(g, total):
-            start = pl.multiple_of(g * (GROUP * SLAB), GROUP * SLAB)
-            slabs = [u[c, :, pl.ds(start + i * SLAB, SLAB)] for i in range(GROUP + 2)]
+            start = g * (GROUP * SLAB)
+            slabs = [u[c, :, start + i * SLAB : start + (i + 1) * SLAB] for i in range(GROUP + 2)]
             stacked = jnp.concatenate(slabs[1:-1], axis=0)
-            flat = jnp.dot(stacked, weave[:, 0:SLAB], preferred_element_type=F32)
+            flat = jnp.dot(stacked, weave[:, first : first + SLAB], preferred_element_type=F32)
             if c > 0:
                 lone = jnp.dot(
                     stacked, weave[:, c * SLAB : (c + 1) * SLAB], preferred_element_type=F32
                 )
             for i in range(GROUP):
                 lower, here, upper = [slabs[i + k].astype(F32) for k in range(3)]
-                along_x = 2.0 * here - upper - lower
                 rest = flat[i * ROWS : (i + 1) * ROWS]
-                special = along_x if c == 0 else lone[i * ROWS : (i + 1) * ROWS]
-                applied = (scale * (along_x + rest) + extra * special).astype(BF16)
+                if c == 0:
+                    applied = both * (2.0 * here - (lower + upper)) + scale * rest
+                else:
+                    lone_part = lone[i * ROWS : (i + 1) * ROWS]
+                    applied = scale * (rest - (lower + upper)) + extra * lone_part
                 total = total + lax.dot_general(
-                    slabs[i + 1], applied, TRANS, preferred_element_type=F32
+                    slabs[i + 1], applied.astype(BF16), TRANS, preferred_element_type=F32
                 )
             return total
 
-        return lax.fori_loop(0, BX // GROUP, group, total)
+        for g in range(BX // GROUP):
+            total = group(g, total)
+        return total
 
     shape = (NV, LANES)
 
@@ -231,6 +243,21 @@
     total = stencil(1, total)
     pass_on(3)
 
+    total = stencil(2, total)
+    v_of = iota(shape, 0)
+    w_of = iota(shape, 1)
+    limit = by_sub(counts[0], counts[1], shape)
+    inside = (v_of < limit) & (lax.rem(w_of, NV) < limit)
+    block = by_sub(total[0:NV], total[NV:ROWS], shape)
+    send1[pl.ds(0, NV, stride=8), :] = jnp.where(inside, block, 0.0)
+
+    swap, values = pairing(1 - gx, 0)
+    for move in moves[0]:
+        move.wait_recv()
+    weights = [jnp.where(by_row, values[0][c], values[1][c]) for c in range(3)]
+    full = couple(lambda c: near[0, c], lambda c: far[0, c], weights)
+    send1[pl.ds(1, NV, stride=8), :] = matched(full, swap)
+
     _, values = pairing(3 - gy, 1)
     keep_here = keep_last[:, 0:LANES]
     weights = [jnp.where(keep_here, values[1][c], values[0][c]) for c in range(3)]
@@ -250,31 +277,6 @@
     )
     back.start()
 
-    total = stencil(2, total)
-    v_of = iota(shape, 0)
-    w_of = iota(shape, 1)
-    limit = by_sub(counts[0], counts[1], shape)
-    inside = (v_of < limit) & (lax.rem(w_of, NV) < limit)
-    block = by_sub(total[0:NV], total[NV:ROWS], shape)
-    send1[pl.ds(0, NV, stride=8), :] = jnp.where(inside, block, 0.0)
-
-    swap, values = pairing(1 - gx, 0)
-    for move in moves[0]:
-        move.wait_recv()
-    weights = [jnp.where(by_row, values[0][c], values[1][c]) for c in range(3)]
-    full = couple(lambda c: near[0, c], lambda c: far[0, c], weights)
-    send1[pl.ds(1, NV, stride=8), :] = matched(full, swap)
-
-    back.wait_recv()
-    packed = back_in[...]
-    turned = pltpu.roll(packed, NV, 1)
-    given = jnp.concatenate(
-        [by_sub(packed, turned, packed.shape), by_sub(turned, packed, packed.shape)], axis=0
-    )
-    send1[pl.ds(2, NV, stride=8), :] = by_sub(
-        jnp.where(keep_here, given, kept), jnp.where(keep_here, kept, given), shape
-    )
-
     swap, values = pairing(4, 2)
     for move in moves[2]:
         move.wait_recv()
@@ -285,12 +287,22 @@
     full = couple(lambda c: far[1, c], lambda c: near[1, c], weights)
     send1[pl.ds(4, NV, stride=8), :] = matched(full, swap)
 
+    back.wait_recv()
+    packed = back_in[...]
+    turned = pltpu.roll(packed, NV, 1)
+    given = jnp.concatenate(
+        [by_sub(packed, turned, packed.shape), by_sub(turned, packed, packed.shape)], axis=0
+    )
+    send1[pl.ds(2, NV, stride=8), :] = by_sub(
+        jnp.where(keep_here, given, kept), jnp.where(keep_here, kept, given), shape
+    )
+
     def exchange(phase, source, target):
         def post(k, carry):
-            ring = k // 8
-            step = (ring + 1) // 2
-            ring = PEERS // 16 + step * (2 * lax.rem(ring, 2) - 1)
-            peer = lax.rem(gz // 8 + ring, 8) * 8 + lax.rem(gz + k + 1, 8)
+            ring = k >> 3
+            step = (ring + 1) >> 1
+            ring = 4 + step * (2 * (ring & 1) - 1)
+            peer = (((plane + ring) & 7) << 3) + ((gz + k + 1) & 7)
             pltpu.make_async_remote_copy(
                 src_ref=source.at[pl.ds(pl.multiple_of(peer * 8, 8), TILE)],
                 dst_ref=target.at[pl.ds(pl.multiple_of(gz * 8, 8), TILE)],
@@ -301,7 +313,7 @@
             ).start()
             return carry
 
-        lax.fori_loop(0, PEERS - 1, post, 0)
+        lax.fori_loop(0, PEERS - 1, post, 0, unroll=UNROLL_POST)
         mine = pl.ds(pl.multiple_of(gz * 8, 8), 8)
         target[mine, :] = source[mine, :]
 
@@ -312,7 +324,7 @@
             dst_ref=target.at[pl.ds(0, size)],
             send_sem=a2a_send.at[phase],
             recv_sem=a2a_recv.at[phase],
-            device_id={"gz": lax.rem(gz + 1, PEERS)},
+            device_id={"gz": after},
             device_id_type=MESH,
         )
 
@@ -397,7 +409,7 @@
         out_specs=vmem,
         scratch_shapes=[
             pltpu.VMEM((3, ROWS, CELLS + 2 * SLAB), BF16),
-            pltpu.VMEM((SLAB, 3 * SLAB), BF16),
+            pltpu.VMEM((SLAB, 4 * SLAB), BF16),
             pltpu.VMEM((8 * SLAB, 3 * LANES), BF16),
             pltpu.VMEM((3, 3, ROWS, SLAB), BF16),
             pltpu.VMEM((2, 3, ROWS, SLAB), BF16),

time: 38.5 us -> 37.8 us (0.982)
  Pallas kernels: 36.7 us -> 35.8 us
    pallas_call x1, Pallas kernels: 36.7 us -> 35.8 us  [per_device(): pl.pallas_call(kernel, out_shape=jax.ShapeDtypeStruct((7, 2, CELLS), F32)...]
where the time goes in v4:
time: 37.8 us; the launch traced here: 37.4 us
  Pallas kernels  35.8 us (95%)
  local copies, waits for them, and re-layouts  1.64 us (4%)
    pallas_call x1, Pallas kernels, per_device(): pl.pallas_call(kernel, out_shape=jax.ShapeDtypeStruct((7, 2, CELLS), F32)...  35.8 us
    unnamed x1, local copies, waits for them, and re-layouts  1.64 us

profile of v4, /device:TPU:4, one launch (start us, length us, event | category | flops | bytes accessed | tf_op | source)
XLA Modules:
  0.0 37.4 jit_solution(11107339850159205935)
XLA Ops:
  0.0 35.8 %assemble.1 = f32[7,2,4096]{2,1,0:T(2,128)} custom-call(bf16[2,3,64,4096]{3,2,1,0:T(8,128)(2,1)} %zvecs.1, s32[2]{0:T(128)} %counts.1, s32[2,6]{1,0:T(2,128)} %adjacency.1, s32[512]{0:T(512)} %mat_id.1, f32[16]{0:T(128)} %shear.1, f32[16]{0:T(128)} %ratio.1, s32[1,128]{1,0:T(1,128)} %owner.1), custom_call_target="tpu_custom_call" | custom-call | tf_op jit(solution)/shard_map/assemble/pallas_call | solution.py:405
  35.8 1.6 %copy.9 = f32[1,2,7,4096]{3,1,2,0:T(2,128)} copy(f32[1,2,7,4096]{3,1,2,0:T(2,128)} %bitcast.3) | data formatting | bytes 458752

commit v5 on v4

--- a/solution.py
+++ b/solution.py
@@ -365,14 +365,20 @@
         send2[pl.ds(b, PEERS, stride=8), :] = by_sub(full[0:NV], full[NV:ROWS], shape)
 
     exchange(1, send2, recv2)
+    whole(1, send2, recv2).wait_recv()
+    out[...] = recv2[...]
+    for move in moves[0] + moves[1] + moves[2] + [back, whole(0, send1, recv1), whole(1, send2, recv2)]:
+        move.wait_send()
+
+
+def lay_out(recv2, out):
+    gx, gy = lax.axis_index("gx"), lax.axis_index("gy")
     tile = (8, LANES)
     b_of = iota(tile, 0)
     x_at, y_at = 2 - gx, 4 - gy
     plain = (b_of == 0) | ((b_of == x_at) & (gx == 1))
     once = ((b_of == x_at) & (gx == 0)) | ((b_of == y_at) & (gy == 1))
     twice = ((b_of == y_at) & (gy == 0)) | (b_of > 4)
-    whole(1, send2, recv2).wait_recv()
-
     def place(m, carry):
         pair = [recv2[pl.ds(pl.multiple_of((2 * m + i) * 8, 8), 8), :] for i in range(2)]
         turned = [pltpu.roll(t, NV, 1) for t in pair]
@@ -392,8 +398,6 @@
         return carry
 
     lax.fori_loop(0, CELLS // LANES, place, 0, unroll=4)
-    for move in moves[0] + moves[1] + moves[2] + [back, whole(0, send1, recv1), whole(1, send2, recv2)]:
-        move.wait_send()
 
 
 TILE = 5
@@ -404,7 +408,7 @@
     vmem = pl.BlockSpec(memory_space=pltpu.VMEM)
     rows = pl.pallas_call(
         kernel,
-        out_shape=jax.ShapeDtypeStruct((7, 2, CELLS), F32),
+        out_shape=pltpu.VMEM((PEERS * 8, LANES), F32),
         in_specs=[pl.BlockSpec(memory_space=pl.ANY), smem, smem, smem, smem, smem, vmem],
         out_specs=vmem,
         scratch_shapes=[
@@ -432,6 +436,13 @@
         compiler_params=pltpu.CompilerParams(collective_id=0, has_side_effects=True),
         name="assemble",
     )(zvecs, counts, adjacency, mat_id, shear, ratio, owner_map)
+    rows = pl.pallas_call(
+        lay_out,
+        out_shape=jax.ShapeDtypeStruct((7, 2, CELLS), F32),
+        in_specs=[vmem],
+        out_specs=vmem,
+        name="lay_out",
+    )(pltpu.with_memory_space_constraint(rows, pltpu.VMEM))
     return jnp.transpose(rows, (1, 0, 2))[None]
 
 

time: 37.8 us -> 36.2 us (0.958)
  local copies, waits for them, and re-layouts: 1.64 us -> 0 us
    unnamed x1 -> x0, local copies, waits for them, and re-layouts: 1.64 us -> none
    pallas_call x1 -> x2, Pallas kernels: 35.8 us -> 35.8 us  [the longest x1 34.4 us: per_device(): pl.pallas_call(kernel, out_shape=pltpu.VMEM((PEERS * 8, LANES), F32), in_...]
where the time goes in v5:
time: 36.2 us; the launch traced here: 35.8 us
  Pallas kernels  35.8 us (99%)
    pallas_call x1, Pallas kernels, per_device(): pl.pallas_call(kernel, out_shape=pltpu.VMEM((PEERS * 8, LANES), F32), in_...  34.4 us
    pallas_call x1, Pallas kernels, per_device(): pl.pallas_call(lay_out, out_shape=jax.ShapeDtypeStruct((7, 2, CELLS), F32...  1.46 us

profile of v5, /device:TPU:4, one launch (start us, length us, event | category | flops | bytes accessed | tf_op | source)
XLA Modules:
  0.0 35.8 jit_solution(416175045238783700)
XLA Ops:
  0.0 34.4 %assemble.1.recv2 = f32[512,128]{1,0:T(8,128)S(1)} custom-call(bf16[2,3,64,4096]{3,2,1,0:T(8,128)(2,1)} %zvecs.1, s32[2]{0:T(128)} %counts.1, s32[2,6]{1,0:T(2,128)} %adjacency.1, s32[512]{0:T(512)} %mat_id.1, f32[16]{0:T(128)} %shear.1, f32[16]{0:T(128)} %ratio.1, s32[1,128]{1,0:T(1,128)} %owner.1), custom_call_target="tpu_custom_call" | custom-call | tf_op jit(solution)/shard_map/assemble/pallas_call | solution.py:409
  34.4 1.5 %lay_out.1 = f32[7,2,4096]{2,1,0:T(2,128)} custom-call(f32[512,128]{1,0:T(8,128)S(1)} %assemble.1.recv2), custom_call_target="tpu_custom_call" | custom-call | tf_op jit(solution)/shard_map/lay_out/pallas_call | solution.py:439

commit v6 on v5

--- a/solution.py
+++ b/solution.py
@@ -134,8 +134,7 @@
         u[c, :, SLAB + CELLS : 2 * SLAB + CELLS] = zero_slab
         loads[2 * c].wait()
         loads[2 * c + 1].wait()
-        layer_y, layer_z, layer_low = layers(c, 0, 3)
-        near[1, c] = layer_low.astype(BF16)
+        layer_y, layer_z = layers(c, 0, 2)
         near_y[0, c] = jnp.where(keep_last, layer_y[NV:ROWS], layer_y[0:NV]).astype(BF16)
         near_y[1, c] = jnp.where(keep_last, layer_y[0:NV], layer_y[NV:ROWS]).astype(BF16)
         near[2, c] = layer_z.astype(BF16)
@@ -239,6 +238,8 @@
 
     pass_on(1)
     total = stencil(0, jnp.zeros((ROWS, ROWS), F32))
+    for c in range(3):
+        near[1, c] = layers(c, 2, 3)[0].astype(BF16)
     pass_on(2)
     total = stencil(1, total)
     pass_on(3)
@@ -397,7 +398,7 @@
             out[:, p, pl.ds(pl.multiple_of(m * LANES, LANES), LANES)] = value[0:7]
         return carry
 
-    lax.fori_loop(0, CELLS // LANES, place, 0, unroll=4)
+    lax.fori_loop(0, CELLS // LANES, place, 0, unroll=16)
 
 
 TILE = 5

time: 36.2 us -> 35.8 us (0.989)
  Pallas kernels: 35.8 us -> 35.4 us
    pallas_call x1, Pallas kernels: 1.46 us -> 1.02 us  [per_device(): pl.pallas_call(lay_out, out_shape=jax.ShapeDtypeStruct((7, 2, CELLS), F32...]
where the time goes in v6:
time: 35.8 us; the launch traced here: 35.4 us
  Pallas kernels  35.4 us (99%)
    pallas_call x1, Pallas kernels, per_device(): pl.pallas_call(kernel, out_shape=pltpu.VMEM((PEERS * 8, LANES), F32), in_...  34.4 us
    pallas_call x1, Pallas kernels, per_device(): pl.pallas_call(lay_out, out_shape=jax.ShapeDtypeStruct((7, 2, CELLS), F32...  1.02 us

profile of v6, /device:TPU:4, one launch (start us, length us, event | category | flops | bytes accessed | tf_op | source)
XLA Modules:
  0.0 35.4 jit_solution(464074624939205529)
XLA Ops:
  0.0 34.4 %assemble.1.recv2 = f32[512,128]{1,0:T(8,128)S(1)} custom-call(bf16[2,3,64,4096]{3,2,1,0:T(8,128)(2,1)} %zvecs.1, s32[2]{0:T(128)} %counts.1, s32[2,6]{1,0:T(2,128)} %adjacency.1, s32[512]{0:T(512)} %mat_id.1, f32[16]{0:T(128)} %shear.1, f32[16]{0:T(128)} %ratio.1, s32[1,128]{1,0:T(1,128)} %owner.1), custom_call_target="tpu_custom_call" | custom-call | tf_op jit(solution)/shard_map/assemble/pallas_call | solution.py:410
  34.4 1.0 %lay_out.1 = f32[7,2,4096]{2,1,0:T(2,128)} custom-call(f32[512,128]{1,0:T(8,128)S(1)} %assemble.1.recv2), custom_call_target="tpu_custom_call" | custom-call | tf_op jit(solution)/shard_map/lay_out/pallas_call | solution.py:440
